TPU v7x, 256 devices: a whole 4x4x8 slice. The times are simulated.
256 devices in a mesh: gz: 64 (over z, y, x_hi), gy: 4 (over x_lo, core).
Axes of the slice: x: 4 (x_hi: 2, x_lo: 2; x = x_hi * 2 + x_lo), y: 4, z: 8, core: 2. Of those that a mesh axis runs over, the one named last changes fastest.
Arguments:
- test_vectors: float32 [4, 256, 384, 256], P(None, 'gz', 'gy'), may hold values from -18 to 18
- conductivity: float32 [256, 384, 256], P('gz', 'gy'), may hold values from 0.1 to 10
Outputs:
- prolongator: float32 [4, 256, 384, 256], P(None, 'gz', 'gy')
- coarse_factors: float32 [10, 64, 96, 64], P(None, 'gz', 'gy')
All inputs are finite; a program needn't handle non-finite values.
Results may differ from a plain program's by a relative error of at most 0.0003.
Values sent between devices are 32-bit elements; how exact they have to be, the bound alone decides.
A program may use at most 64 MiB of HBM per device.

v0:
```python
import jax
import jax.numpy as jnp
from jax import lax
from jax.sharding import PartitionSpec as P

RELAX_WEIGHT = 2.0 / 3.0
PAIR_LIST = ((0, 0), (0, 1), (0, 2), (0, 3), (1, 1), (1, 2), (1, 3), (2, 2), (2, 3), (3, 3))


def extended(array, sides, width):
    for axis, dim in sides:
        devices, length = (lax.axis_size(axis), array.shape[dim])
        up = [(i, (i + 1) % devices) for i in range(devices)]
        down = [(j, i) for i, j in up]
        last = lax.slice_in_dim(array, length - width, length, axis=dim)
        leading = lax.slice_in_dim(array, 0, width, axis=dim)
        before = lax.ppermute(last, axis, up)
        after = lax.ppermute(leading, axis, down)
        array = jnp.concatenate([before, array, after], axis=dim)
    return array


def from_behind(array, axis, by):
    devices = lax.axis_size(axis)
    return lax.ppermute(array, axis, [(i, (i + by) % devices) for i in range(devices)])


def sweep(values_ext, coef_ext):
    center_coef = coef_ext[1:-1, 1:-1]
    center_vals = values_ext[:, 1:-1, 1:-1]
    neighbours = [
        (coef_ext[2:, 1:-1], values_ext[:, 2:, 1:-1]),
        (coef_ext[:-2, 1:-1], values_ext[:, :-2, 1:-1]),
        (coef_ext[1:-1, 2:], values_ext[:, 1:-1, 2:]),
        (coef_ext[1:-1, :-2], values_ext[:, 1:-1, :-2]),
        (jnp.roll(center_coef, -1, axis=-1), jnp.roll(center_vals, -1, axis=-1)),
        (jnp.roll(center_coef, 1, axis=-1), jnp.roll(center_vals, 1, axis=-1)),
    ]
    diagonal = jnp.zeros_like(center_coef)
    fluxes = jnp.zeros_like(center_vals)
    for next_coef, next_vals in neighbours:
        weight = 2.0 * center_coef * next_coef / (center_coef + next_coef)
        diagonal = diagonal + weight
        fluxes = fluxes + weight * (center_vals - next_vals)
    return center_vals - RELAX_WEIGHT * fluxes / diagonal


def block_table(across):
    cells = jnp.arange(across) // 4
    return (cells[:, None] == jnp.arange(across // 4)[None, :]).astype(jnp.float32)


def pair_products(fields):
    return jnp.stack([fields[left_idx] * fields[right_idx] for left_idx, right_idx in PAIR_LIST])


def block_sums(values):
    number, layers, height, across = values.shape
    folded = values.reshape(number, layers // 4, 4, height // 4, 4, across).sum(axis=(2, 4))
    flat = jnp.dot(folded.reshape(-1, across), block_table(across), precision=lax.Precision.HIGHEST)
    return flat.reshape(number, layers // 4, height // 4, across // 4)


def spread_blocks(values, across):
    number, layers, height, blocks_x = values.shape
    flat = jnp.dot(
        values.reshape(-1, blocks_x), block_table(across).T, precision=lax.Precision.HIGHEST
    )
    spread = flat.reshape(number, layers, height, across)
    spread = jnp.repeat(spread, 4, axis=1)
    return jnp.repeat(spread, 4, axis=2)


def factor(blocks, grams):
    matrix = [[None] * 4 for _ in range(4)]
    for position, pair in enumerate(PAIR_LIST):
        matrix[pair[0]][pair[1]] = grams[position]
    trace = matrix[0][0] + matrix[1][1] + matrix[2][2] + matrix[3][3]
    ridge = 0.64 * (trace / 256.0 + 1e-06)
    upper = [[None] * 4 for _ in range(4)]
    for row_index in range(4):
        for col_index in range(row_index, 4):
            accum = matrix[row_index][col_index]
            if row_index == col_index:
                accum = accum + ridge
            for inner_index in range(row_index):
                accum = accum - upper[inner_index][row_index] * upper[inner_index][col_index]
            if row_index == col_index:
                upper[row_index][row_index] = jnp.sqrt(accum)
            else:
                upper[row_index][col_index] = accum / upper[row_index][row_index]
    listed = jnp.stack([upper[pair[0]][pair[1]] for pair in PAIR_LIST])
    inverse_list = jnp.stack(
        [
            1.0 / upper[pair[0]][pair[1]] if pair[0] == pair[1] else upper[pair[0]][pair[1]]
            for pair in PAIR_LIST
        ]
    )
    spread = spread_blocks(inverse_list, blocks.shape[3])
    lookup = {}
    for position, pair in enumerate(PAIR_LIST):
        lookup[pair] = spread[position]
    columns = []
    for col_index in range(4):
        accum = blocks[col_index]
        for inner_index in range(col_index):
            accum = accum - lookup[inner_index, col_index] * columns[inner_index]
        columns.append(accum * lookup[col_index, col_index])
    return (jnp.stack(columns), listed)


def factorize(region, scales):
    scaled = region * scales[:, None, None, None]
    grams = block_sums(pair_products(scaled))
    return factor(scaled, grams)


def body(test_vectors, conductivity):
    stacked = jnp.concatenate((test_vectors, conductivity[None]), axis=0)
    padded = extended(stacked, (("gz", 1), ("gy", 2)), 1)
    coef_ext = padded[4]
    first = sweep(padded[:4], coef_ext)
    second_pad = extended(first, (("gz", 1), ("gy", 2)), 1)
    relaxed = sweep(second_pad, coef_ext)
    squares = jnp.sum(relaxed * relaxed, axis=(1, 2, 3))
    cell_total = (
        relaxed.shape[1]
        * lax.axis_size("gz")
        * relaxed.shape[2]
        * lax.axis_size("gy")
        * relaxed.shape[3]
    )
    totals = lax.psum(squares, ("gz", "gy"))
    scales = lax.rsqrt(totals / cell_total + 1e-06)
    rolled = jnp.roll(relaxed, -2, axis=3)
    lead_planes = from_behind(rolled[:, :2], "gz", -1)
    z_region = jnp.concatenate((rolled[:, 2:], lead_planes), axis=1)
    lead_rows = from_behind(z_region[:, :, :2], "gy", -1)
    region = jnp.concatenate((z_region[:, :, 2:], lead_rows), axis=2)
    prolong_ext, factors = factorize(region, scales)
    back_rows = from_behind(prolong_ext[:, :, -2:], "gy", 1)
    y_cells = jnp.concatenate((back_rows, prolong_ext[:, :, :-2]), axis=2)
    back_planes = from_behind(y_cells[:, -2:], "gz", 1)
    cells = jnp.concatenate((back_planes, y_cells[:, :-2]), axis=1)
    return (jnp.roll(cells, 2, axis=3), factors)


def solution(mesh):
    return jax.shard_map(
        body,
        mesh=mesh,
        in_specs=(P(None, "gz", "gy", None), P("gz", "gy", None)),
        out_specs=(P(None, "gz", "gy", None), P(None, "gz", "gy", None)),
        check_vma=False,
    )
```

profile of v0, /device:TPU:1, one launch (start us, length us, event | category | flops | bytes accessed | tf_op | source)
XLA Modules:
  0.0 219.3 jit_solution(6840498802866061804)
XLA Ops:
  0.6 1.4 pad_maximum_fusion.31
  2.1 3.6 %collective-permute-start = (f32[5,1,96,256]{3,2,1,0:T(8,128)S(1)}, f32[5,1,96,256]{3,2,1,0:T(8,128)S(1)}, u32[]{:S(2)}, u32[]{:S(2)}) collective-permute-start(f32[5,1,96,256]{3,2,1,0:T(8,128)S(1)} %get-tuple-element.33), channel_id=1, source_target_pairs={{0,4},{4,8},{8,12},{12,16},{16,20},{20,24},{24,28},{28,32},{32,36}... | collective-permute-start | bytes 1474568 | tf_op jit(solution)/shard_map/ppermute | solution.py:17
  5.7 7.8 %collective-permute-start.1 = (f32[5,1,96,256]{3,2,1,0:T(8,128)S(1)}, f32[5,1,96,256]{3,2,1,0:T(8,128)S(1)}, u32[]{:S(2)}, u32[]{:S(2)}) collective-permute-start(f32[5,1,96,256]{3,2,1,0:T(8,128)S(1)} %get-tuple-element.34), channel_id=1, source_target_pairs={{4,0},{8,4},{12,8},{16,12},{20,16},{24,20},{28,24},{32,28},{36,32}... | collective-permute-start | bytes 1474568 | tf_op jit(solution)/shard_map/ppermute | solution.py:18
  13.6 0.6 fusion.61
  14.1 12.0 %collective-permute-done = f32[5,1,96,256]{3,2,1,0:T(8,128)S(1)} collective-permute-done((f32[5,1,96,256]{3,2,1,0:T(8,128)S(1)}, f32[5,1,96,256]{3,2,1,0:T(8,128)S(1)}, u32[]{:S(2)}, u32[]{:S(2)}) %collective-permute-start) | collective-permute-done | bytes 491552 | tf_op jit(solution)/shard_map/ppermute | solution.py:17
  26.2 2.0 collective-permute-done.1
  28.2 2.7 %collective-permute-start.2 = (f32[5,6,1,256]{3,2,1,0:T(1,128)S(1)}, f32[5,6,1,256]{3,2,1,0:T(1,128)S(1)}, u32[]{:S(2)}, u32[]{:S(2)}) collective-permute-start(f32[5,6,1,256]{3,2,1,0:T(1,128)S(1)} %get-tuple-element.28), channel_id=1, source_target_pairs={{0,1},{1,2},{2,3},{3,0},{4,5},{5,6},{6,7},{7,4},{8,9},{9,10},{10,1... | collective-permute-start | bytes 92168 | tf_op jit(solution)/shard_map/ppermute | solution.py:17
  30.9 0.3 fusion.60
  31.2 0.7 collective-permute-done.2
  31.9 2.3 %collective-permute-done.3 = f32[5,6,1,256]{3,2,1,0:T(1,128)S(1)} collective-permute-done((f32[5,6,1,256]{3,2,1,0:T(1,128)S(1)}, f32[5,6,1,256]{3,2,1,0:T(1,128)S(1)}, u32[]{:S(2)}, u32[]{:S(2)}) %collective-permute-start.3) | collective-permute-done | bytes 30752 | tf_op jit(solution)/shard_map/ppermute | solution.py:18
  34.6 0.5 add_add_fusion
  35.1 2.8 %fusion.25 = f32[4,4,96,256]{3,2,1,0:T(8,128)S(1)} fusion(f32[4,4,96,256]{3,2,1,0:T(8,128)S(1)} %copy-done, f32[5,6,1,256]{3,2,1,0:T(1,128)S(1)} %collective-permute-done.2, f32[5,1,96,256]{3,2,1,0:T(8,128)S(1)} %collective-permute-done.1, f32[5,1,96,256]{3,2,1,0:T(8,128)S(1)} %collective-permute-done, f32[1,4,96,256]{3,2,1,0:T(8,128)S(1)} %bitcast.72, ...), kind=kLoop, calls=%fused_computation.39 | loop fusion | flops 13369344 | bytes 10481664 | tf_op jit(solution)/shard_map/sub | solution.py:45
  37.9 7.2 %collective-permute-start.4 = (f32[4,1,96,256]{3,2,1,0:T(8,128)S(1)}, f32[4,1,96,256]{3,2,1,0:T(8,128)S(1)}, u32[]{:S(2)}, u32[]{:S(2)}) collective-permute-start(f32[4,1,96,256]{3,2,1,0:T(8,128)S(1)} %get-tuple-element.48), channel_id=1, source_target_pairs={{4,0},{8,4},{12,8},{16,12},{20,16},{24,20},{28,24},{32,28},{36,32}... | collective-permute-start | bytes 1179656 | tf_op jit(solution)/shard_map/ppermute | solution.py:18
  45.2 0.5 fusion.58
  45.7 7.2 %collective-permute-done.4 = f32[4,1,96,256]{3,2,1,0:T(8,128)S(1)} collective-permute-done((f32[4,1,96,256]{3,2,1,0:T(8,128)S(1)}, f32[4,1,96,256]{3,2,1,0:T(8,128)S(1)}, u32[]{:S(2)}, u32[]{:S(2)}) %collective-permute-start.4) | collective-permute-done | bytes 393248 | tf_op jit(solution)/shard_map/ppermute | solution.py:18
  53.0 8.0 %collective-permute-done.5 = f32[4,1,96,256]{3,2,1,0:T(8,128)S(1)} collective-permute-done((f32[4,1,96,256]{3,2,1,0:T(8,128)S(1)}, f32[4,1,96,256]{3,2,1,0:T(8,128)S(1)}, u32[]{:S(2)}, u32[]{:S(2)}) %collective-permute-start.5) | collective-permute-done | bytes 393248 | tf_op jit(solution)/shard_map/ppermute | solution.py:17
  61.1 1.7 collective-permute-start.7
  62.8 0.3 fusion.59
  63.1 1.2 collective-permute-done.6
  64.3 3.1 %multiply_reduce_fusion = (f32[4]{0:T(128)S(1)}, f32[4,4,96,256]{3,2,1,0:T(8,128)S(1)}) fusion(f32[4,4,96,256]{3,2,1,0:T(8,128)S(1)} %fusion.25, f32[4,96,256]{2,1,0:T(8,128)S(1)} %get-tuple-element.20, f32[4,4,96,255]{3,2,1,0:T(8,128)S(1)} %get-tuple-element.50, f32[4,4,96,1]{3,2,1,0:T(8,128)S(1)} %get-tuple-element.52, ...), kind=kLoop, calls=%fused_computation.72 | loop fusion | flops 12582908 | bytes 9879568 | tf_op jit(solution)/shard_map/reduce_sum | solution.py:125
  67.4 0.5 slice.419
  68.0 0.3 fusion.39
  68.3 7.8 %collective-permute-start.8 = (f32[4,2,96,256]{3,2,1,0:T(8,128)S(1)}, f32[4,2,96,256]{3,2,1,0:T(8,128)S(1)}, u32[]{:S(2)}, u32[]{:S(2)}) collective-permute-start(f32[4,2,96,256]{3,2,1,0:T(8,128)S(1)} %get-tuple-element.30), channel_id=1, source_target_pairs={{0,252},{4,0},{8,4},{12,8},{16,12},{20,16},{24,20},{28,24},{32,28}... | collective-permute-start | bytes 2359304 | tf_op jit(solution)/shard_map/ppermute | solution.py:25
  76.1 86.0 %psum.7 = f32[4]{0:T(128)S(1)} all-reduce(f32[4]{0:T(128)S(1)} %get-tuple-element.18), channel_id=1, replica_groups=mesh['gz'=64,'gy'=4] {'gz','gy'}, use_global_device_ids=true, to_apply=%region_1.2 | all-reduce | flops 4 | bytes 32 | tf_op jit(solution)/shard_map/psum | solution.py:133
  162.2 0.7 collective-permute-start.9
  163.1 2.7 %collective-permute-done.9 = f32[4,4,2,256]{3,2,1,0:T(2,128)S(1)} collective-permute-done((f32[4,4,2,256]{3,2,1,0:T(2,128)S(1)}, f32[4,4,2,256]{3,2,1,0:T(2,128)S(1)}, u32[]{:S(2)}, u32[]{:S(2)}) %collective-permute-start.9) | collective-permute-done | bytes 32800 | tf_op jit(solution)/shard_map/ppermute | solution.py:25
  166.0 1.6 slice_multiply_fusion
  167.6 1.1 stack.94
  168.7 0.8 constant_dynamic-update-slice_fusion.9
  169.4 1.9 stack.95
  171.3 1.9 stack.96
  173.2 1.9 stack.97
  175.1 0.9 stack.98
  176.4 1.1 stack.103
  177.5 1.8 constant_dynamic-update-slice_fusion.8
  179.4 1.8 constant_dynamic-update-slice_fusion.7
  181.2 0.8 constant_dynamic-update-slice_fusion.6
  182.0 0.8 constant_dynamic-update-slice_fusion.5
  182.7 0.8 constant_dynamic-update-slice_fusion.4
  183.5 0.8 constant_dynamic-update-slice_fusion.3
  184.3 0.8 constant_dynamic-update-slice_fusion.2
  185.1 0.8 constant_dynamic-update-slice_fusion.1
  185.8 0.8 constant_dynamic-update-slice_fusion
  186.6 3.3 %reduce_sum.19 = f32[10,24,256]{2,1,0:T(8,128)S(1)} reduce(f32[10,1,4,24,4,256]{5,4,3,2,1,0:T(4,128)} %constant_dynamic-update-slice_fusion, f32[]{:T(128)} %constant.28.clone.1), dimensions={1,2,4}, to_apply=%region_2.3 | reduce | flops 921600 | bytes 4177924 | tf_op jit(solution)/shard_map/reduce_sum | solution.py:59
  192.9 1.2 collective-permute-done.10
  194.4 2.5 %collective-permute-start.11 = (f32[4,2,96,256]{3,2,1,0:T(8,128)S(1)}, f32[4,2,96,256]{3,2,1,0:T(8,128)S(1)}, u32[]{:S(2)}, u32[]{:S(2)}) collective-permute-start(f32[4,2,96,256]{3,2,1,0:T(8,128)S(1)} %get-tuple-element.35), channel_id=1, source_target_pairs={{0,4},{4,8},{8,12},{12,16},{16,20},{20,24},{24,28},{28,32},{32,36}... | collective-permute-start | bytes 2359304 | tf_op jit(solution)/shard_map/ppermute | solution.py:25
  196.9 20.4 %collective-permute-done.11 = f32[4,2,96,256]{3,2,1,0:T(8,128)S(1)} collective-permute-done((f32[4,2,96,256]{3,2,1,0:T(8,128)S(1)}, f32[4,2,96,256]{3,2,1,0:T(8,128)S(1)}, u32[]{:S(2)}, u32[]{:S(2)}) %collective-permute-start.11) | collective-permute-done | bytes 786464 | tf_op jit(solution)/shard_map/ppermute | solution.py:25
  217.6 1.6 fusion
  (93 shorter events, 4.6 us)
Async XLA Ops:
  0.6 12.9 %copy-start = (f32[4,4,96,256]{3,2,1,0:T(8,128)S(1)}, f32[4,4,96,256]{3,2,1,0:T(8,128)}, u32[]{:S(2)}) copy-start(f32[4,4,96,256]{3,2,1,0:T(8,128)} %param.2) | copy-start | bytes 4718596
  2.1 24.1 %collective-permute-start = (f32[5,1,96,256]{3,2,1,0:T(8,128)S(1)}, f32[5,1,96,256]{3,2,1,0:T(8,128)S(1)}, u32[]{:S(2)}, u32[]{:S(2)}) collective-permute-start(f32[5,1,96,256]{3,2,1,0:T(8,128)S(1)} %get-tuple-element.33), channel_id=1, source_target_pairs={{0,4},{4,8},{8,12},{12,16},{16,20},{20,24},{24,28},{28,32},{32,36}... | collective-permute-start | bytes 1474568 | tf_op jit(solution)/shard_map/ppermute | solution.py:17
  5.7 22.4 %copy-start.1 = (f32[4,96,256]{2,1,0:T(8,128)S(1)}, f32[4,96,256]{2,1,0:T(8,128)}, u32[]{:S(2)}) copy-start(f32[4,96,256]{2,1,0:T(8,128)} %param.3) | copy-start | bytes 1179652
  5.7 22.4 %collective-permute-start.1 = (f32[5,1,96,256]{3,2,1,0:T(8,128)S(1)}, f32[5,1,96,256]{3,2,1,0:T(8,128)S(1)}, u32[]{:S(2)}, u32[]{:S(2)}) collective-permute-start(f32[5,1,96,256]{3,2,1,0:T(8,128)S(1)} %get-tuple-element.34), channel_id=1, source_target_pairs={{4,0},{8,4},{12,8},{16,12},{20,16},{24,20},{28,24},{32,28},{36,32}... | collective-permute-start | bytes 1474568 | tf_op jit(solution)/shard_map/ppermute | solution.py:18
  28.2 3.7 %collective-permute-start.2 = (f32[5,6,1,256]{3,2,1,0:T(1,128)S(1)}, f32[5,6,1,256]{3,2,1,0:T(1,128)S(1)}, u32[]{:S(2)}, u32[]{:S(2)}) collective-permute-start(f32[5,6,1,256]{3,2,1,0:T(1,128)S(1)} %get-tuple-element.28), channel_id=1, source_target_pairs={{0,1},{1,2},{2,3},{3,0},{4,5},{5,6},{6,7},{7,4},{8,9},{9,10},{10,1... | collective-permute-start | bytes 92168 | tf_op jit(solution)/shard_map/ppermute | solution.py:17
  30.9 3.3 %collective-permute-start.3 = (f32[5,6,1,256]{3,2,1,0:T(1,128)S(1)}, f32[5,6,1,256]{3,2,1,0:T(1,128)S(1)}, u32[]{:S(2)}, u32[]{:S(2)}) collective-permute-start(f32[5,6,1,256]{3,2,1,0:T(1,128)S(1)} %get-tuple-element.27), channel_id=1, source_target_pairs={{1,0},{2,1},{3,2},{0,3},{5,4},{6,5},{7,6},{4,7},{9,8},{10,9},{11,1... | collective-permute-start | bytes 92168 | tf_op jit(solution)/shard_map/ppermute | solution.py:18
  37.9 15.0 %collective-permute-start.4 = (f32[4,1,96,256]{3,2,1,0:T(8,128)S(1)}, f32[4,1,96,256]{3,2,1,0:T(8,128)S(1)}, u32[]{:S(2)}, u32[]{:S(2)}) collective-permute-start(f32[4,1,96,256]{3,2,1,0:T(8,128)S(1)} %get-tuple-element.48), channel_id=1, source_target_pairs={{4,0},{8,4},{12,8},{16,12},{20,16},{24,20},{28,24},{32,28},{36,32}... | collective-permute-start | bytes 1179656 | tf_op jit(solution)/shard_map/ppermute | solution.py:18
  45.2 15.8 %collective-permute-start.5 = (f32[4,1,96,256]{3,2,1,0:T(8,128)S(1)}, f32[4,1,96,256]{3,2,1,0:T(8,128)S(1)}, u32[]{:S(2)}, u32[]{:S(2)}) collective-permute-start(f32[4,1,96,256]{3,2,1,0:T(8,128)S(1)} %get-tuple-element.47), channel_id=1, source_target_pairs={{0,4},{4,8},{8,12},{12,16},{16,20},{20,24},{24,28},{28,32},{32,36}... | collective-permute-start | bytes 1179656 | tf_op jit(solution)/shard_map/ppermute | solution.py:17
  61.0 3.3 %collective-permute-start.6 = (f32[4,6,1,256]{3,2,1,0:T(1,128)S(1)}, f32[4,6,1,256]{3,2,1,0:T(1,128)S(1)}, u32[]{:S(2)}, u32[]{:S(2)}) collective-permute-start(f32[4,6,1,256]{3,2,1,0:T(1,128)S(1)} %get-tuple-element.31), channel_id=1, source_target_pairs={{1,0},{2,1},{3,2},{0,3},{5,4},{6,5},{7,6},{4,7},{9,8},{10,9},{11,1... | collective-permute-start | bytes 73736 | tf_op jit(solution)/shard_map/ppermute | solution.py:18
  61.1 3.2 %collective-permute-start.7 = (f32[4,6,1,256]{3,2,1,0:T(1,128)S(1)}, f32[4,6,1,256]{3,2,1,0:T(1,128)S(1)}, u32[]{:S(2)}, u32[]{:S(2)}) collective-permute-start(f32[4,6,1,256]{3,2,1,0:T(1,128)S(1)} %get-tuple-element.32), channel_id=1, source_target_pairs={{0,1},{1,2},{2,3},{3,0},{4,5},{5,6},{6,7},{7,4},{8,9},{9,10},{10,1... | collective-permute-start | bytes 73736 | tf_op jit(solution)/shard_map/ppermute | solution.py:17
  68.3 93.9 %collective-permute-start.8 = (f32[4,2,96,256]{3,2,1,0:T(8,128)S(1)}, f32[4,2,96,256]{3,2,1,0:T(8,128)S(1)}, u32[]{:S(2)}, u32[]{:S(2)}) collective-permute-start(f32[4,2,96,256]{3,2,1,0:T(8,128)S(1)} %get-tuple-element.30), channel_id=1, source_target_pairs={{0,252},{4,0},{8,4},{12,8},{16,12},{20,16},{24,20},{28,24},{32,28}... | collective-permute-start | bytes 2359304 | tf_op jit(solution)/shard_map/ppermute | solution.py:25
  162.2 3.6 %collective-permute-start.9 = (f32[4,4,2,256]{3,2,1,0:T(2,128)S(1)}, f32[4,4,2,256]{3,2,1,0:T(2,128)S(1)}, u32[]{:S(2)}, u32[]{:S(2)}) collective-permute-start(f32[4,4,2,256]{3,2,1,0:T(2,128)S(1)} %pad_maximum_fusion.35), channel_id=1, source_target_pairs={{0,3},{1,0},{2,1},{3,2},{4,7},{5,4},{6,5},{7,6},{8,11},{9,8},{10,9... | collective-permute-start | bytes 98312 | tf_op jit(solution)/shard_map/ppermute | solution.py:25
  169.4 5.6 %copy-start.4 = (f32[1,4,96,256]{3,2,1,0:T(8,128)S(1)}, f32[1,4,96,256]{3,2,1,0:T(8,128)}, u32[]{:S(2)}) copy-start(f32[1,4,96,256]{3,2,1,0:T(8,128)} %get-tuple-element.38) | copy-start | bytes 1179652
  177.5 3.7 %copy-start.3 = (f32[1,1,4,24,4,256]{5,4,3,2,1,0:T(4,128)S(1)}, f32[1,1,4,24,4,256]{5,4,3,2,1,0:T(4,128)}, u32[]{:S(2)}) copy-start(f32[1,1,4,24,4,256]{5,4,3,2,1,0:T(4,128)} %stack.97) | copy-start | bytes 1179652
  177.5 4.4 %copy-start.2 = (f32[1,1,4,24,4,256]{5,4,3,2,1,0:T(4,128)S(1)}, f32[1,1,4,24,4,256]{5,4,3,2,1,0:T(4,128)}, u32[]{:S(2)}) copy-start(f32[1,1,4,24,4,256]{5,4,3,2,1,0:T(4,128)} %stack.98) | copy-start | bytes 1179652
  192.9 1.3 collective-permute-start.10
  194.4 22.9 %collective-permute-start.11 = (f32[4,2,96,256]{3,2,1,0:T(8,128)S(1)}, f32[4,2,96,256]{3,2,1,0:T(8,128)S(1)}, u32[]{:S(2)}, u32[]{:S(2)}) collective-permute-start(f32[4,2,96,256]{3,2,1,0:T(8,128)S(1)} %get-tuple-element.35), channel_id=1, source_target_pairs={{0,4},{4,8},{8,12},{12,16},{16,20},{20,24},{24,28},{28,32},{32,36}... | collective-permute-start | bytes 2359304 | tf_op jit(solution)/shard_map/ppermute | solution.py:25
  196.9 22.3 %copy-start.5 = (f32[10,1,24,64]{3,2,1,0:T(8,128)}, f32[10,1,24,64]{3,2,1,0:T(8,128)S(1)}, u32[]{:S(2)}) copy-start(f32[10,1,24,64]{3,2,1,0:T(8,128)S(1)} %constant_dynamic-update-slice_fusion.20) | copy-start | bytes 184324
where the time goes:
time: 221 us; the launch traced here: 219 us
  blocking collectives  86 us (39%)
  waiting for transfers between devices  57.8 us (26%)
  starting transfers between devices  34.4 us (16%)
  local copies, waits for them, and re-layouts  23.2 us (10%)
  other arithmetic  16.1 us (7%)
    psum x1, blocking collectives, body(): totals = lax.psum(squares, ('gz', 'gy'))  86 us
    ppermute x4, waiting for transfers between devices, from_behind(): lax.ppermute(array, axis, [(i, (i + by) % devices) for i in range(devices)])  24.3 us
    ppermute x4, waiting for transfers between devices, extended(): before = lax.ppermute(last, axis, up)  20.7 us
    ppermute x4, starting transfers between devices, extended(): after = lax.ppermute(leading, axis, down)  15.2 us
    ppermute x4, waiting for transfers between devices, extended(): after = lax.ppermute(leading, axis, down)  12.8 us
    ppermute x4, starting transfers between devices, from_behind(): lax.ppermute(array, axis, [(i, (i + by) % devices) for i in range(devices)])  11.1 us
    another operation x11, local copies, waits for them, and re-layouts, pair_products(): jnp.stack([fields[left_idx] * fields[right_idx] for left_idx, right_idx i...  9.93 us
    unnamed x32, local copies, waits for them, and re-layouts  9.12 us
  transfers between devices with their start and end apart: 12, of which 10 were waited for; matrix products, arithmetic and copies ran while one was open for 1% of the time, Pallas kernels for 0%

commit v1 on v0

v1 whole, which is shorter than its diff:
```python
import functools

import jax
import jax.numpy as jnp
from jax import lax
from jax.experimental import pallas as pl
from jax.experimental.pallas import tpu as pltpu
from jax.sharding import PartitionSpec as P

MESH = pl.DeviceIdType.MESH
F32 = jnp.float32
KEEP = 1.0 / 3.0
STEP = 2.0 / 3.0
PAIRS = ((0, 0), (0, 1), (0, 2), (0, 3), (1, 1), (1, 2), (1, 3), (2, 2), (2, 3), (3, 3))
AT = {pair: i for i, pair in enumerate(PAIRS)}
ROWS = 96
ACROSS = 256
PAD = 8
TILES = ROWS // 8
CHUNK_TILES = 3
CHUNKS = TILES // CHUNK_TILES
CHUNK_ROWS = CHUNK_TILES * 8
ORDER = (0, 3, 1, 2)
N_GZ = 64
N_GY = 4
CELLS = 256 * 384 * 256


def device(z, y, x_hi, x_lo, core):
    return (z * 8 + y * 2 + x_hi, x_lo * 2 + core)


def sum_partners():
    gz, gy = lax.axis_index("gz"), lax.axis_index("gy")
    z, y, x_hi = gz // 8, lax.rem(gz, 8) // 2, lax.rem(gz, 2)
    x_lo, core = gy // 2, lax.rem(gy, 2)
    chip = [device(z, y, x_hi, x_lo, 1 - core)]
    plane = [
        device(z, lax.rem(y + dy, 4), lax.rem(x_hi + dh, 2), lax.rem(x_lo + dl, 2), core)
        for dy in range(4)
        for dh in range(2)
        for dl in range(2)
        if dy or dh or dl
    ]
    column = [device(lax.rem(z + dz, 8), y, x_hi, x_lo, core) for dz in range(1, 8)]
    return chip, plane, column


SUM_SIZES = (1, 15, 7)
SUM_BASE = (0, 1, 16)


def kernel(
    tv_hbm, k_hbm, out_hbm, fac_ref,
    tv, kc, tz, kz, f, fz, wn, r, prod, gsum, mine, zrecv, full, spread,
    ysend, yrecv, fysend, fyrecv, esend, erecv, sum_send, sum_recv,
    load_sem, out_sem, az_send, az_recv, akz_send, akz_recv, bz_send, bz_recv,
    ay_send, ay_recv, by_send, by_recv, gz_send, gz_recv, ey_send, ey_recv,
    s_send, s_recv,
):
    gz, gy = lax.axis_index("gz"), lax.axis_index("gy")
    z_dev = (
        (lax.rem(gz + N_GZ - 1, N_GZ), gy),
        (lax.rem(gz + 1, N_GZ), gy),
    )
    y_dev = (
        (gz, lax.rem(gy + N_GY - 1, N_GY)),
        (gz, lax.rem(gy + 1, N_GY)),
    )
    partners = sum_partners()

    def remote(src, dst, send_sem, recv_sem, to):
        return pltpu.make_async_remote_copy(
            src_ref=src, dst_ref=dst, send_sem=send_sem, recv_sem=recv_sem,
            device_id=to, device_id_type=MESH,
        )

    loads = [
        pltpu.make_async_copy(tv_hbm, tv.at[:, :, pl.ds(PAD, ROWS), :], load_sem.at[0]),
        pltpu.make_async_copy(k_hbm, kc.at[:, pl.ds(PAD, ROWS), :], load_sem.at[1]),
    ]
    for copy in loads:
        copy.start()

    barrier = pltpu.get_barrier_semaphore()
    greeted = list(z_dev) + list(y_dev) + [d for group in partners for d in group]
    for to in greeted:
        pl.semaphore_signal(barrier, inc=1, device_id=to, device_id_type=MESH)

    for copy in loads:
        copy.wait()
    for side, row in ((0, PAD), (1, PAD + ROWS - 1)):
        for p in range(4):
            for v in range(4):
                ysend[side, pl.ds(v * 4 + p, 1), :] = tv[v, p, pl.ds(row, 1), :]
            ysend[side, pl.ds(16 + p, 1), :] = kc[p, pl.ds(row, 1), :]
    for field in range(20):
        for side in range(2):
            prod[field, side, pl.ds(ROWS, 8), :] = jnp.zeros((8, 128), F32)
        gsum[field, pl.ds(24, 8), :] = jnp.zeros((8, ACROSS), F32)

    pl.semaphore_wait(barrier, len(greeted))

    face = (0, 3)
    az, akz = {}, {}
    for c in ORDER:
        rows = pl.ds(c * CHUNK_ROWS, CHUNK_ROWS)
        for side in range(2):
            az[c, side] = remote(
                tv_hbm.at[:, face[side], rows, :], tz.at[1 - side, :, rows, :],
                az_send.at[side, c], az_recv.at[1 - side, c], z_dev[side],
            )
            akz[c, side] = remote(
                k_hbm.at[face[side], rows, :], kz.at[1 - side, rows, :],
                akz_send.at[side, c], akz_recv.at[1 - side, c], z_dev[side],
            )
            akz[c, side].start()
            az[c, side].start()
        if c == ORDER[0]:
            ay = [
                remote(ysend.at[side], yrecv.at[1 - side], ay_send.at[side],
                       ay_recv.at[1 - side], y_dev[side])
                for side in range(2)
            ]
            for copy in ay:
                copy.start()

    for copy in ay:
        copy.wait()
    for side, row in ((0, PAD - 1), (1, PAD + ROWS)):
        for p in range(4):
            for v in range(4):
                tv[v, p, pl.ds(row, 1), :] = yrecv[side, pl.ds(v * 4 + p, 1), :]
            kc[p, pl.ds(row, 1), :] = yrecv[side, pl.ds(16 + p, 1), :]

    def left(x):
        return pltpu.roll(x, 1, 1)

    def right(x):
        return pltpu.roll(x, ACROSS - 1, 1)

    def weights(t, p):
        at = t * 8
        here = kc[p, pl.ds(at + PAD, 8), :]
        near = (
            kc[p + 1, pl.ds(at + PAD, 8), :] if p < 3 else kz[1, pl.ds(at, 8), :],
            kc[p - 1, pl.ds(at + PAD, 8), :] if p > 0 else kz[0, pl.ds(at, 8), :],
            kc[p, pl.ds(at + PAD + 1, 8), :],
            kc[p, pl.ds(at + PAD - 1, 8), :],
            right(here),
            left(here),
        )
        parts = [n / (here + n) for n in near]
        total = ((parts[0] + parts[1]) + (parts[2] + parts[3])) + (parts[4] + parts[5])
        norm = STEP / total
        for i in range(6):
            wn[i, p, pl.ds(at, 8), :] = parts[i] * norm

    def relax(t, p, src, halo):
        at = t * 8
        w = [wn[i, p, pl.ds(at, 8), :] for i in range(6)]
        result = []
        for v in range(4):
            here = src[v, p, pl.ds(at + PAD, 8), :]
            up = src[v, p + 1, pl.ds(at + PAD, 8), :] if p < 3 else halo[1, v, pl.ds(at, 8), :]
            down = src[v, p - 1, pl.ds(at + PAD, 8), :] if p > 0 else halo[0, v, pl.ds(at, 8), :]
            ahead = src[v, p, pl.ds(at + PAD + 1, 8), :]
            behind = src[v, p, pl.ds(at + PAD - 1, 8), :]
            total = (w[0] * up + w[1] * down) + (w[2] * ahead + w[3] * behind)
            total = total + (w[4] * right(here) + w[5] * left(here))
            result.append(here * KEEP + total)
        return result

    def first_tile(t, p):
        for v, value in enumerate(relax(t, p, tv, tz)):
            f[v, p, pl.ds(t * 8 + PAD, 8), :] = value

    def second_tile(t, p):
        for v, value in enumerate(relax(t, p, f, fz)):
            r[v, p, pl.ds(t * 8, 8), :] = value

    for t in range(TILES):
        for p in (1, 2):
            weights(t, p)
            first_tile(t, p)

    bz = {}
    done = []
    for c in ORDER:
        rows = pl.ds(c * CHUNK_ROWS, CHUNK_ROWS)
        rows_in = pl.ds(c * CHUNK_ROWS + PAD, CHUNK_ROWS)
        for side in range(2):
            akz[c, side].wait()
            az[c, side].wait()
        for t in range(c * CHUNK_TILES, (c + 1) * CHUNK_TILES):
            for p in face:
                weights(t, p)
                first_tile(t, p)
        for side in range(2):
            bz[c, side] = remote(
                f.at[:, face[side], rows_in, :], fz.at[1 - side, :, rows, :],
                bz_send.at[side, c], bz_recv.at[1 - side, c], z_dev[side],
            )
            bz[c, side].start()
        done.append(c)
        if len(done) == 2:
            for side, row in ((0, PAD), (1, PAD + ROWS - 1)):
                for p in range(4):
                    for v in range(4):
                        fysend[side, pl.ds(v * 4 + p, 1), :] = f[v, p, pl.ds(row, 1), :]
            by = [
                remote(fysend.at[side], fyrecv.at[1 - side], by_send.at[side],
                       by_recv.at[1 - side], y_dev[side])
                for side in range(2)
            ]
            for copy in by:
                copy.start()

    for copy in by:
        copy.wait()
    for side, row in ((0, PAD - 1), (1, PAD + ROWS)):
        for p in range(4):
            for v in range(4):
                f[v, p, pl.ds(row, 1), :] = fyrecv[side, pl.ds(v * 4 + p, 1), :]
    for t in range(TILES):
        for p in (1, 2):
            second_tile(t, p)

    squares = [jnp.zeros((8, ACROSS), F32) for _ in range(4)]
    for c in ORDER:
        for side in range(2):
            bz[c, side].wait()
        for t in range(c * CHUNK_TILES, (c + 1) * CHUNK_TILES):
            rows = pl.ds(t * 8, 8)
            for half in range(2):
                second_tile(t, face[half])
                low = [r[v, 2 * half, rows, :] for v in range(4)]
                high = [r[v, 2 * half + 1, rows, :] for v in range(4)]
                for i, (a, b) in enumerate(PAIRS):
                    value = low[a] * low[b] + high[a] * high[b]
                    prod[half * 10 + i, 0, rows, :] = value[:, :128]
                    prod[half * 10 + i, 1, rows, :] = value[:, 128:]
                    if a == b:
                        squares[a] = squares[a] + value

    def exchange(stage):
        sends = []
        for i, to in enumerate(partners[stage]):
            at = SUM_BASE[stage] + i
            copy = remote(sum_send.at[stage], sum_recv.at[at], s_send.at[at], s_recv.at[at], to)
            copy.start()
            sends.append(copy)
        return sends

    def collect(stage, sends):
        total = sum_send[stage]
        for i, copy in enumerate(sends):
            copy.wait()
            total = total + sum_recv[SUM_BASE[stage] + i]
        return total

    for v in range(4):
        both = squares[v][:, :128] + squares[v][:, 128:]
        sum_send[0, pl.ds(v, 1), :] = jnp.sum(both, axis=0, keepdims=True)
    sum_send[0, pl.ds(4, 4), :] = jnp.zeros((4, 128), F32)
    sends = exchange(0)

    for field in range(20):
        for side in range(2):
            own = pl.ds(side * 128, 128)
            parts = [prod[field, side, pl.ds(2 + i, 24, stride=4), :] for i in range(4)]
            gsum[field, pl.ds(0, 24), own] = (parts[0] + parts[1]) + (parts[2] + parts[3])
            gsum[field, pl.ds(24, 1), own] = (
                prod[field, side, pl.ds(0, 1), :] + prod[field, side, pl.ds(1, 1), :]
            )
    cell = lax.rem(lax.broadcasted_iota(jnp.int32, (ACROSS, 128), 0) + ACROSS - 2, ACROSS) // 4
    lane = lax.broadcasted_iota(jnp.int32, (ACROSS, 128), 1)
    pick_low = (cell == lane).astype(F32)
    pick_high = (cell + 64 == lane).astype(F32)
    for half in range(2):
        a = gsum[pl.ds(half * 10, 5), :, :].reshape(160, ACROSS)
        b = gsum[pl.ds(half * 10 + 5, 5), :, :].reshape(160, ACROSS)
        packed = jnp.dot(a, pick_low, precision=lax.Precision.HIGHEST, preferred_element_type=F32)
        packed = packed + jnp.dot(
            b, pick_high, precision=lax.Precision.HIGHEST, preferred_element_type=F32
        )
        mine[half] = packed.reshape(5, 32, 128)
    gz_copies = [
        remote(mine.at[half], zrecv.at[1 - half], gz_send.at[half], gz_recv.at[1 - half], z_dev[half])
        for half in range(2)
    ]
    for copy in gz_copies:
        copy.start()

    sum_send[1] = collect(0, sends)
    sends = exchange(1)
    sum_send[2] = collect(1, sends)
    sends = exchange(2)

    for copy in gz_copies:
        copy.wait()
    for half in range(2):
        total = mine[half] + zrecv[half]
        full[half] = total
        for i in range(5):
            esend[0, pl.ds(half * 5 + i, 1), :] = total[i, 24:25]
            esend[1, pl.ds(half * 5 + i, 1), :] = total[i, 23:24]
    ey = [
        remote(esend.at[side], erecv.at[1 - side], ey_send.at[side], ey_recv.at[1 - side], y_dev[side])
        for side in range(2)
    ]
    for copy in ey:
        copy.start()
    for copy in ey:
        copy.wait()
    for half in range(2):
        for i in range(5):
            n = half * 5 + i
            full[half, i, pl.ds(24, 1), :] = esend[0, pl.ds(n, 1), :] + erecv[0, pl.ds(n, 1), :]
            full[half, i, pl.ds(23, 1), :] = esend[1, pl.ds(n, 1), :] + erecv[1, pl.ds(n, 1), :]

    lanes = lax.broadcasted_iota(jnp.int32, (32, 128), 1)
    is_low = lanes < 64
    gram = [None] * 10
    for i in range(5):
        low, high = full[0, i], full[1, i]
        gram[i] = jnp.where(is_low, low, pltpu.roll(high, 64, 1))
        gram[i + 5] = jnp.where(is_low, pltpu.roll(low, 64, 1), high)

    across = lax.broadcasted_iota(jnp.int32, (128, 2 * ACROSS), 1)
    owner = lax.rem(lax.rem(across, ACROSS) + ACROSS - 2, ACROSS) // 4 + (across // ACROSS) * 64
    expand = (lax.broadcasted_iota(jnp.int32, (128, 2 * ACROSS), 0) == owner).astype(F32)

    totals = jnp.sum(collect(2, sends), axis=1, keepdims=True)
    scale_col = lax.rsqrt(totals / CELLS + 1e-06)
    scale = [jnp.broadcast_to(scale_col[v : v + 1, :], (32, 128)) for v in range(4)]

    m = {pair: gram[i] * (scale[pair[0]] * scale[pair[1]]) for i, pair in enumerate(PAIRS)}
    trace = (m[0, 0] + m[1, 1]) + (m[2, 2] + m[3, 3])
    ridge = 0.64 * (trace / 256.0 + 1e-06)
    upper, inverse = {}, []
    for i in range(4):
        for j in range(i, 4):
            value = m[i, j]
            if i == j:
                value = value + ridge
            for n in range(i):
                value = value - upper[n, i] * upper[n, j]
            if i == j:
                upper[i, i] = jnp.sqrt(value)
                inverse.append(1.0 / upper[i, i])
            else:
                upper[i, j] = value * inverse[i]
    table = []
    for n, (i, j) in enumerate(PAIRS):
        fac_ref[n, 0] = pltpu.roll(upper[i, j], 64, 1)[:24, :64]
        table.append((scale[j] if i == j else upper[i, j]) * inverse[j])
    stacked = jnp.concatenate(table, axis=0)
    wide = jnp.dot(stacked, expand, precision=lax.Precision.HIGHEST, preferred_element_type=F32)
    spread[...] = wide.reshape(10, 32, 2 * ACROSS)

    sub = lax.broadcasted_iota(jnp.int32, (8, ACROSS), 0)
    before, after = sub < 2, sub >= 6
    outs = []
    for c in range(CHUNKS):
        for t in range(c * CHUNK_TILES, (c + 1) * CHUNK_TILES):
            rows = pl.ds(t * 8, 8)
            for half in range(2):
                columns = pl.ds(half * ACROSS, ACROSS)
                field = []
                for n in range(10):
                    one = spread[n, pl.ds(24 if t == 0 else 2 * t - 1, 1), columns]
                    two = spread[n, pl.ds(2 * t, 1), columns]
                    three = spread[n, pl.ds(2 * t + 1, 1), columns]
                    field.append(jnp.where(before, one, jnp.where(after, three, two)))
                for p in (2 * half, 2 * half + 1):
                    done_columns = []
                    for j in range(4):
                        value = r[j, p, rows, :] * field[AT[j, j]]
                        for i in range(j):
                            value = value - field[AT[i, j]] * done_columns[i]
                        done_columns.append(value)
                        r[j, p, rows, :] = value
        rows = pl.ds(c * CHUNK_ROWS, CHUNK_ROWS)
        copy = pltpu.make_async_copy(r.at[:, :, rows, :], out_hbm.at[:, :, rows, :], out_sem.at[c])
        copy.start()
        outs.append(copy)
    for copy in outs:
        copy.wait()


def body(test_vectors, conductivity):
    vm = lambda *shape: pltpu.VMEM(shape, F32)
    dma = lambda *shape: pltpu.SemaphoreType.DMA(shape)
    return pl.pallas_call(
        kernel,
        out_shape=(
            jax.ShapeDtypeStruct((4, 4, ROWS, ACROSS), F32),
            jax.ShapeDtypeStruct((10, 1, 24, 64), F32),
        ),
        in_specs=[pl.BlockSpec(memory_space=pl.ANY)] * 2,
        out_specs=(
            pl.BlockSpec(memory_space=pl.ANY),
            pl.BlockSpec(memory_space=pltpu.VMEM),
        ),
        scratch_shapes=[
            vm(4, 4, ROWS + 2 * PAD, ACROSS),
            vm(4, ROWS + 2 * PAD, ACROSS),
            vm(2, 4, ROWS, ACROSS),
            vm(2, ROWS, ACROSS),
            vm(4, 4, ROWS + 2 * PAD, ACROSS),
            vm(2, 4, ROWS, ACROSS),
            vm(6, 4, ROWS, ACROSS),
            vm(4, 4, ROWS, ACROSS),
            vm(20, 2, ROWS + 8, 128),
            vm(20, 32, ACROSS),
            vm(2, 5, 32, 128),
            vm(2, 5, 32, 128),
            vm(2, 5, 32, 128),
            vm(10, 32, 2 * ACROSS),
            vm(2, 24, ACROSS),
            vm(2, 24, ACROSS),
            vm(2, 16, ACROSS),
            vm(2, 16, ACROSS),
            vm(2, 16, 128),
            vm(2, 16, 128),
            vm(3, 8, 128),
            vm(23, 8, 128),
            dma(2), dma(CHUNKS),
            dma(2, CHUNKS), dma(2, CHUNKS), dma(2, CHUNKS), dma(2, CHUNKS),
            dma(2, CHUNKS), dma(2, CHUNKS),
            dma(2), dma(2), dma(2), dma(2), dma(2), dma(2), dma(2), dma(2),
            dma(23), dma(23),
        ],
        compiler_params=pltpu.CompilerParams(collective_id=0, has_side_effects=True),
        name="bootstrap",
    )(test_vectors, conductivity)


def solution(mesh):
    return jax.shard_map(
        body,
        mesh=mesh,
        in_specs=(P(None, "gz", "gy", None), P("gz", "gy", None)),
        out_specs=(P(None, "gz", "gy", None), P(None, "gz", "gy", None)),
        check_vma=False,
    )
```

time: 221 us -> 71.8 us (0.32)
  blocking collectives: 86 us -> 0 us
  Pallas kernels: 0 us -> 67.6 us
  waiting for transfers between devices: 57.8 us -> 0 us
  starting transfers between devices: 34.4 us -> 0 us
  local copies, waits for them, and re-layouts: 23.2 us -> 3.38 us
  other arithmetic: 16.1 us -> 0 us
    psum x1 -> x0, blocking collectives: 86 us -> none  [body(): totals = lax.psum(squares, ('gz', 'gy'))]
    pallas_call x0 -> x1, Pallas kernels: none -> 67.6 us  [body(): pl.pallas_call(kernel, out_shape=(jax.ShapeDtypeStruct((4, 4, ROWS, ACROS...]
    ppermute x12 -> x0, waiting for transfers between devices: 57.8 us -> none  [the longest x4 24.3 us: from_behind(): lax.ppermute(array, axis, [(i, (i + by) % devices) for i in range(devices)])]
    ppermute x12 -> x0, starting transfers between devices: 34.4 us -> none  [the longest x4 15.2 us: extended(): after = lax.ppermute(leading, axis, down)]
    another operation x27 -> x0, local copies, waits for them, and re-layouts: 10.8 us -> none  [the longest x11 9.93 us: pair_products(): jnp.stack([fields[left_idx] * fields[right_idx] for left_idx, right_idx i...]
    reduce_sum x2 -> x0, other arithmetic: 6.44 us -> none  [the longest x1 3.34 us: block_sums(): values.reshape(number, layers // 4, 4, height // 4, 4, across)]
    unnamed x32 -> x4, local copies, waits for them, and re-layouts: 9.12 us -> 3.38 us
    sub x1 -> x0, other arithmetic: 2.76 us -> none  [sweep(): return center_vals - RELAX_WEIGHT * fluxes / diagonal]
  transfers between devices with their start and end apart: 12 -> 0, of which waited for: 10 -> 0; matrix products, arithmetic and copies ran while one was open for 1% -> 0% of each run, Pallas kernels for 0% -> 0%
where the time goes in v1:
time: 71.8 us; the launch traced here: 71.7 us
  Pallas kernels  67.6 us (94%)
  local copies, waits for them, and re-layouts  3.38 us (5%)
    pallas_call x1, Pallas kernels, body(): pl.pallas_call(kernel, out_shape=(jax.ShapeDtypeStruct((4, 4, ROWS, ACROS...  67.6 us
    unnamed x4, local copies, waits for them, and re-layouts  3.38 us

profile of v1, /device:TPU:1, one launch (start us, length us, event | category | flops | bytes accessed | tf_op | source)
XLA Modules:
  0.0 71.7 jit_solution(5648627283058012115)
XLA Ops:
  0.6 67.6 %bootstrap.1 = (f32[4,4,96,256]{3,2,1,0:T(8,128)}, f32[10,1,24,64]{3,2,1,0:T(8,128)}) custom-call(f32[4,4,96,256]{3,2,1,0:T(8,128)} %tv_hbm.1, f32[4,96,256]{2,1,0:T(8,128)} %k_hbm.1), custom_call_target="tpu_custom_call" | custom-call | tf_op jit(solution)/shard_map/bootstrap/pallas_call | solution.py:395
  68.3 0.0 copy-start
  68.3 2.7 %copy.6 = f32[4,4,96,256]{3,2,1,0:T(8,128)} copy(f32[4,4,96,256]{3,2,1,0:T(8,128)} %get-tuple-element.4) | data formatting | bytes 3145728
  71.0 0.0 copy-done
  71.0 0.6 copy.7
Async XLA Ops:
  68.3 2.7 %copy-start = (f32[10,1,24,64]{3,2,1,0:T(8,128)S(1)}, f32[10,1,24,64]{3,2,1,0:T(8,128)}, u32[]{:S(2)}) copy-start(f32[10,1,24,64]{3,2,1,0:T(8,128)} %get-tuple-element.5) | copy-start | bytes 184324

commit v2 on v1

--- a/solution.py
+++ b/solution.py
@@ -13,14 +13,14 @@
 STEP = 2.0 / 3.0
 PAIRS = ((0, 0), (0, 1), (0, 2), (0, 3), (1, 1), (1, 2), (1, 3), (2, 2), (2, 3), (3, 3))
 AT = {pair: i for i, pair in enumerate(PAIRS)}
+BF16 = jnp.bfloat16
 ROWS = 96
 ACROSS = 256
 PAD = 8
 TILES = ROWS // 8
-CHUNK_TILES = 3
-CHUNKS = TILES // CHUNK_TILES
-CHUNK_ROWS = CHUNK_TILES * 8
-ORDER = (0, 3, 1, 2)
+CHUNKS = ((0, 3), (8, 4), (3, 3), (6, 2))
+EARLY = 88
+LATE = 40
 N_GZ = 64
 N_GY = 4
 CELLS = 256 * 384 * 256
@@ -43,20 +43,34 @@
         if dy or dh or dl
     ]
     column = [device(lax.rem(z + dz, 8), y, x_hi, x_lo, core) for dz in range(1, 8)]
-    return chip, plane, column
-
-
-SUM_SIZES = (1, 15, 7)
-SUM_BASE = (0, 1, 16)
+    return chip, column, plane
+
+
+SUM_BASE = (0, 1, 8)
+
+
+def spans():
+    return [(c, tile * 8, tiles * 8) for c, (tile, tiles) in enumerate(CHUNKS)]
+
+
+def split_dot(x, table):
+    high = x.astype(BF16)
+    rest = x - high.astype(F32)
+    middle = rest.astype(BF16)
+    low = (rest - middle.astype(F32)).astype(BF16)
+    one = jnp.dot(low, table, preferred_element_type=F32)
+    two = jnp.dot(middle, table, preferred_element_type=F32)
+    return (one + two) + jnp.dot(high, table, preferred_element_type=F32)
 
 
 def kernel(
-    tv_hbm, k_hbm, out_hbm, fac_ref,
-    tv, kc, tz, kz, f, fz, wn, r, prod, gsum, mine, zrecv, full, spread,
+    tv_hbm, k_hbm, r, gram_early, gram_late, total_ref,
+    tv, kc, tz, kz, f, fz, wn, prod, sum_early, sum_late,
+    mine_early, mine_late, from_early, from_late,
     ysend, yrecv, fysend, fyrecv, esend, erecv, sum_send, sum_recv,
-    load_sem, out_sem, az_send, az_recv, akz_send, akz_recv, bz_send, bz_recv,
-    ay_send, ay_recv, by_send, by_recv, gz_send, gz_recv, ey_send, ey_recv,
-    s_send, s_recv,
+    load_sem, az_send, az_recv, akz_send, akz_recv, bz_send, bz_recv,
+    ay_send, ay_recv, by_send, by_recv, ge_send, ge_recv, gl_send, gl_recv,
+    ey_send, ey_recv, s_send, s_recv,
 ):
     gz, gy = lax.axis_index("gz"), lax.axis_index("gy")
     z_dev = (
@@ -97,14 +111,16 @@
     for field in range(20):
         for side in range(2):
             prod[field, side, pl.ds(ROWS, 8), :] = jnp.zeros((8, 128), F32)
-        gsum[field, pl.ds(24, 8), :] = jnp.zeros((8, ACROSS), F32)
+    for half in range(2):
+        for part in range(2):
+            sum_early[half, part, pl.ds(80, 8), :] = jnp.zeros((8, ACROSS), F32)
 
     pl.semaphore_wait(barrier, len(greeted))
 
     face = (0, 3)
     az, akz = {}, {}
-    for c in ORDER:
-        rows = pl.ds(c * CHUNK_ROWS, CHUNK_ROWS)
+    for c, start, count in spans():
+        rows = pl.ds(start, count)
         for side in range(2):
             az[c, side] = remote(
                 tv_hbm.at[:, face[side], rows, :], tz.at[1 - side, :, rows, :],
@@ -116,7 +132,7 @@
             )
             akz[c, side].start()
             az[c, side].start()
-        if c == ORDER[0]:
+        if c == 0:
             ay = [
                 remote(ysend.at[side], yrecv.at[1 - side], ay_send.at[side],
                        ay_recv.at[1 - side], y_dev[side])
@@ -185,14 +201,13 @@
             first_tile(t, p)
 
     bz = {}
-    done = []
-    for c in ORDER:
-        rows = pl.ds(c * CHUNK_ROWS, CHUNK_ROWS)
-        rows_in = pl.ds(c * CHUNK_ROWS + PAD, CHUNK_ROWS)
+    for c, start, count in spans():
+        rows = pl.ds(start, count)
+        rows_in = pl.ds(start + PAD, count)
         for side in range(2):
             akz[c, side].wait()
             az[c, side].wait()
-        for t in range(c * CHUNK_TILES, (c + 1) * CHUNK_TILES):
+        for t in range(start // 8, (start + count) // 8):
             for p in face:
                 weights(t, p)
                 first_tile(t, p)
@@ -202,8 +217,7 @@
                 bz_send.at[side, c], bz_recv.at[1 - side, c], z_dev[side],
             )
             bz[c, side].start()
-        done.append(c)
-        if len(done) == 2:
+        if c == 1:
             for side, row in ((0, PAD), (1, PAD + ROWS - 1)):
                 for p in range(4):
                     for v in range(4):
@@ -226,11 +240,43 @@
         for p in (1, 2):
             second_tile(t, p)
 
+    def group_sums(field, first_row, into, at):
+        for side in range(2):
+            parts = [prod[field, side, pl.ds(first_row + i, 8, stride=4), :] for i in range(4)]
+            into[field // 10, (field % 10) // 5, pl.ds(at, 8), pl.ds(side * 128, 128)] = (
+                (parts[0] + parts[1]) + (parts[2] + parts[3])
+            )
+
+    cell = ((lax.broadcasted_iota(jnp.int32, (ACROSS, 128), 0) + (ACROSS - 2)) & (ACROSS - 1)) >> 2
+    lane = lax.broadcasted_iota(jnp.int32, (ACROSS, 128), 1)
+    pick = [(cell + 64 * part == lane).astype(F32).astype(BF16) for part in range(2)]
+
+    def pack(sums, half):
+        return split_dot(sums[half, 0], pick[0]) + split_dot(sums[half, 1], pick[1])
+
     squares = [jnp.zeros((8, ACROSS), F32) for _ in range(4)]
-    for c in ORDER:
+    for c, start, count in spans():
+        if c == len(CHUNKS) - 1:
+            for field in range(20):
+                n = field % 5
+                group_sums(field, 2, sum_early, n * 8)
+                group_sums(field, 66, sum_early, 40 + n * 8)
+                for side in range(2):
+                    sum_early[field // 10, (field % 10) // 5, pl.ds(80 + n, 1), pl.ds(side * 128, 128)] = (
+                        prod[field, side, pl.ds(0, 1), :] + prod[field, side, pl.ds(1, 1), :]
+                    )
+            for half in range(2):
+                mine_early[half] = pack(sum_early, half)
+            ge = [
+                remote(mine_early.at[half], from_early.at[1 - half], ge_send.at[half],
+                       ge_recv.at[1 - half], z_dev[half])
+                for half in range(2)
+            ]
+            for copy in ge:
+                copy.start()
         for side in range(2):
             bz[c, side].wait()
-        for t in range(c * CHUNK_TILES, (c + 1) * CHUNK_TILES):
+        for t in range(start // 8, (start + count) // 8):
             rows = pl.ds(t * 8, 8)
             for half in range(2):
                 second_tile(t, face[half])
@@ -253,87 +299,101 @@
         return sends
 
     def collect(stage, sends):
-        total = sum_send[stage]
-        for i, copy in enumerate(sends):
+        for copy in sends:
             copy.wait()
-            total = total + sum_recv[SUM_BASE[stage] + i]
-        return total
-
-    for v in range(4):
-        both = squares[v][:, :128] + squares[v][:, 128:]
-        sum_send[0, pl.ds(v, 1), :] = jnp.sum(both, axis=0, keepdims=True)
-    sum_send[0, pl.ds(4, 4), :] = jnp.zeros((4, 128), F32)
+        total = [sum_send[stage]] + [sum_recv[SUM_BASE[stage] + i] for i in range(len(sends))]
+        while len(total) > 1:
+            total = [sum(total[i : i + 2][1:], total[i]) for i in range(0, len(total), 2)]
+        return total[0]
+
+    stacked = [jnp.sum(q[:, :128] + q[:, 128:], axis=0, keepdims=True) for q in squares]
+    stacked = jnp.concatenate(stacked + [jnp.zeros((4, 128), F32)], axis=0)
+    stacked = jnp.sum(stacked, axis=1, keepdims=True)
+    on_diagonal = lax.broadcasted_iota(jnp.int32, (8, 128), 0) == lax.broadcasted_iota(
+        jnp.int32, (8, 128), 1
+    )
+    sum_send[0] = jnp.sum(jnp.where(on_diagonal, stacked, 0.0), axis=0, keepdims=True)
     sends = exchange(0)
 
     for field in range(20):
-        for side in range(2):
-            own = pl.ds(side * 128, 128)
-            parts = [prod[field, side, pl.ds(2 + i, 24, stride=4), :] for i in range(4)]
-            gsum[field, pl.ds(0, 24), own] = (parts[0] + parts[1]) + (parts[2] + parts[3])
-            gsum[field, pl.ds(24, 1), own] = (
-                prod[field, side, pl.ds(0, 1), :] + prod[field, side, pl.ds(1, 1), :]
-            )
-    cell = lax.rem(lax.broadcasted_iota(jnp.int32, (ACROSS, 128), 0) + ACROSS - 2, ACROSS) // 4
-    lane = lax.broadcasted_iota(jnp.int32, (ACROSS, 128), 1)
-    pick_low = (cell == lane).astype(F32)
-    pick_high = (cell + 64 == lane).astype(F32)
+        group_sums(field, 34, sum_late, (field % 5) * 8)
     for half in range(2):
-        a = gsum[pl.ds(half * 10, 5), :, :].reshape(160, ACROSS)
-        b = gsum[pl.ds(half * 10 + 5, 5), :, :].reshape(160, ACROSS)
-        packed = jnp.dot(a, pick_low, precision=lax.Precision.HIGHEST, preferred_element_type=F32)
-        packed = packed + jnp.dot(
-            b, pick_high, precision=lax.Precision.HIGHEST, preferred_element_type=F32
-        )
-        mine[half] = packed.reshape(5, 32, 128)
-    gz_copies = [
-        remote(mine.at[half], zrecv.at[1 - half], gz_send.at[half], gz_recv.at[1 - half], z_dev[half])
+        mine_late[half] = pack(sum_late, half)
+    gl = [
+        remote(mine_late.at[half], from_late.at[1 - half], gl_send.at[half],
+               gl_recv.at[1 - half], z_dev[half])
         for half in range(2)
     ]
-    for copy in gz_copies:
+    for copy in gl:
         copy.start()
 
     sum_send[1] = collect(0, sends)
     sends = exchange(1)
-    sum_send[2] = collect(1, sends)
-    sends = exchange(2)
-
-    for copy in gz_copies:
+
+    for copy in ge:
         copy.wait()
     for half in range(2):
-        total = mine[half] + zrecv[half]
-        full[half] = total
+        total = mine_early[half] + from_early[half]
+        gram_early[half] = total
+        esend[0, half] = total[80:88]
         for i in range(5):
-            esend[0, pl.ds(half * 5 + i, 1), :] = total[i, 24:25]
-            esend[1, pl.ds(half * 5 + i, 1), :] = total[i, 23:24]
+            esend[1, half, pl.ds(i, 1), :] = total[47 + 8 * i : 48 + 8 * i]
+        esend[1, half, pl.ds(5, 3), :] = jnp.zeros((3, 128), F32)
     ey = [
         remote(esend.at[side], erecv.at[1 - side], ey_send.at[side], ey_recv.at[1 - side], y_dev[side])
         for side in range(2)
     ]
     for copy in ey:
         copy.start()
+
+    sum_send[2] = collect(1, sends)
+    sends = exchange(2)
+
     for copy in ey:
         copy.wait()
     for half in range(2):
+        gram_early[half, pl.ds(80, 8), :] = esend[0, half] + erecv[0, half]
         for i in range(5):
-            n = half * 5 + i
-            full[half, i, pl.ds(24, 1), :] = esend[0, pl.ds(n, 1), :] + erecv[0, pl.ds(n, 1), :]
-            full[half, i, pl.ds(23, 1), :] = esend[1, pl.ds(n, 1), :] + erecv[1, pl.ds(n, 1), :]
-
-    lanes = lax.broadcasted_iota(jnp.int32, (32, 128), 1)
-    is_low = lanes < 64
+            one = pl.ds(i, 1)
+            gram_early[half, pl.ds(47 + 8 * i, 1), :] = esend[1, half, one, :] + erecv[1, half, one, :]
+    for copy in gl:
+        copy.wait()
+    for half in range(2):
+        gram_late[half] = mine_late[half] + from_late[half]
+    total_ref[...] = jnp.broadcast_to(collect(2, sends), (8, 128))
+
+
+def finish(
+    r, gram_early, gram_late, total_ref, out_hbm, fac_hbm, spread, out, fac, out_sem, fac_sem
+):
+    across = lax.broadcasted_iota(jnp.int32, (128, 2 * ACROSS), 1)
+    owner = (((across + (ACROSS - 2)) & (ACROSS - 1)) >> 2) + ((across >> 8) << 6)
+    expand = (lax.broadcasted_iota(jnp.int32, (128, 2 * ACROSS), 0) == owner).astype(F32).astype(BF16)
+
+    is_low = lax.broadcasted_iota(jnp.int32, (32, 128), 1) < 64
+    lane = lax.broadcasted_iota(jnp.int32, (1, 128), 1)
+    scale_row = lax.rsqrt(total_ref[0:1, :] / CELLS + 1e-06)
+    scale = [
+        jnp.sum(jnp.where(lane == v, scale_row, 0.0), axis=1, keepdims=True) for v in range(4)
+    ]
+
+    def groups(half, i):
+        edge = jnp.broadcast_to(gram_early[half, pl.ds(80 + i, 1), :], (8, 128))
+        return jnp.concatenate(
+            [
+                gram_early[half, pl.ds(8 * i, 8), :],
+                gram_late[half, pl.ds(8 * i, 8), :],
+                gram_early[half, pl.ds(40 + 8 * i, 8), :],
+                edge,
+            ],
+            axis=0,
+        )
+
     gram = [None] * 10
     for i in range(5):
-        low, high = full[0, i], full[1, i]
+        low, high = groups(0, i), groups(1, i)
         gram[i] = jnp.where(is_low, low, pltpu.roll(high, 64, 1))
         gram[i + 5] = jnp.where(is_low, pltpu.roll(low, 64, 1), high)
-
-    across = lax.broadcasted_iota(jnp.int32, (128, 2 * ACROSS), 1)
-    owner = lax.rem(lax.rem(across, ACROSS) + ACROSS - 2, ACROSS) // 4 + (across // ACROSS) * 64
-    expand = (lax.broadcasted_iota(jnp.int32, (128, 2 * ACROSS), 0) == owner).astype(F32)
-
-    totals = jnp.sum(collect(2, sends), axis=1, keepdims=True)
-    scale_col = lax.rsqrt(totals / CELLS + 1e-06)
-    scale = [jnp.broadcast_to(scale_col[v : v + 1, :], (32, 128)) for v in range(4)]
 
     m = {pair: gram[i] * (scale[pair[0]] * scale[pair[1]]) for i, pair in enumerate(PAIRS)}
     trace = (m[0, 0] + m[1, 1]) + (m[2, 2] + m[3, 3])
@@ -351,19 +411,19 @@
                 inverse.append(1.0 / upper[i, i])
             else:
                 upper[i, j] = value * inverse[i]
-    table = []
-    for n, (i, j) in enumerate(PAIRS):
-        fac_ref[n, 0] = pltpu.roll(upper[i, j], 64, 1)[:24, :64]
-        table.append((scale[j] if i == j else upper[i, j]) * inverse[j])
-    stacked = jnp.concatenate(table, axis=0)
-    wide = jnp.dot(stacked, expand, precision=lax.Precision.HIGHEST, preferred_element_type=F32)
+    table = [(scale[j] if i == j else upper[i, j]) * inverse[j] for i, j in PAIRS]
+    wide = split_dot(jnp.concatenate(table, axis=0), expand)
     spread[...] = wide.reshape(10, 32, 2 * ACROSS)
+    for n, pair in enumerate(PAIRS):
+        fac[n, 0] = pltpu.roll(upper[pair], 64, 1)[:24, :64]
+    fac_copy = pltpu.make_async_copy(fac, fac_hbm, fac_sem)
+    fac_copy.start()
 
     sub = lax.broadcasted_iota(jnp.int32, (8, ACROSS), 0)
     before, after = sub < 2, sub >= 6
     outs = []
-    for c in range(CHUNKS):
-        for t in range(c * CHUNK_TILES, (c + 1) * CHUNK_TILES):
+    for c in range(4):
+        for t in range(c * 3, c * 3 + 3):
             rows = pl.ds(t * 8, 8)
             for half in range(2):
                 columns = pl.ds(half * ACROSS, ACROSS)
@@ -380,11 +440,12 @@
                         for i in range(j):
                             value = value - field[AT[i, j]] * done_columns[i]
                         done_columns.append(value)
-                        r[j, p, rows, :] = value
-        rows = pl.ds(c * CHUNK_ROWS, CHUNK_ROWS)
-        copy = pltpu.make_async_copy(r.at[:, :, rows, :], out_hbm.at[:, :, rows, :], out_sem.at[c])
+                        out[j, p, rows, :] = value
+        rows = pl.ds(c * 24, 24)
+        copy = pltpu.make_async_copy(out.at[:, :, rows, :], out_hbm.at[:, :, rows, :], out_sem.at[c])
         copy.start()
         outs.append(copy)
+    fac_copy.wait()
     for copy in outs:
         copy.wait()
 
@@ -392,49 +453,69 @@
 def body(test_vectors, conductivity):
     vm = lambda *shape: pltpu.VMEM(shape, F32)
     dma = lambda *shape: pltpu.SemaphoreType.DMA(shape)
-    return pl.pallas_call(
+    shape = lambda *dims: jax.ShapeDtypeStruct(dims, F32)
+    in_vmem = pl.BlockSpec(memory_space=pltpu.VMEM)
+    anywhere = pl.BlockSpec(memory_space=pl.ANY)
+    n = len(CHUNKS)
+    padded = ROWS + 2 * PAD
+    staged = pl.pallas_call(
         kernel,
         out_shape=(
-            jax.ShapeDtypeStruct((4, 4, ROWS, ACROSS), F32),
-            jax.ShapeDtypeStruct((10, 1, 24, 64), F32),
+            shape(4, 4, ROWS, ACROSS),
+            shape(2, EARLY, 128),
+            shape(2, LATE, 128),
+            shape(8, 128),
         ),
-        in_specs=[pl.BlockSpec(memory_space=pl.ANY)] * 2,
-        out_specs=(
-            pl.BlockSpec(memory_space=pl.ANY),
-            pl.BlockSpec(memory_space=pltpu.VMEM),
-        ),
+        in_specs=[pl.BlockSpec(memory_space=pltpu.HBM)] * 2,
+        out_specs=(in_vmem,) * 4,
         scratch_shapes=[
-            vm(4, 4, ROWS + 2 * PAD, ACROSS),
-            vm(4, ROWS + 2 * PAD, ACROSS),
+            vm(4, 4, padded, ACROSS),
+            vm(4, padded, ACROSS),
             vm(2, 4, ROWS, ACROSS),
             vm(2, ROWS, ACROSS),
-            vm(4, 4, ROWS + 2 * PAD, ACROSS),
+            vm(4, 4, padded, ACROSS),
             vm(2, 4, ROWS, ACROSS),
             vm(6, 4, ROWS, ACROSS),
-            vm(4, 4, ROWS, ACROSS),
             vm(20, 2, ROWS + 8, 128),
-            vm(20, 32, ACROSS),
-            vm(2, 5, 32, 128),
-            vm(2, 5, 32, 128),
-            vm(2, 5, 32, 128),
-            vm(10, 32, 2 * ACROSS),
+            vm(2, 2, EARLY, ACROSS),
+            vm(2, 2, LATE, ACROSS),
+            vm(2, EARLY, 128),
+            vm(2, LATE, 128),
+            vm(2, EARLY, 128),
+            vm(2, LATE, 128),
             vm(2, 24, ACROSS),
             vm(2, 24, ACROSS),
             vm(2, 16, ACROSS),
             vm(2, 16, ACROSS),
-            vm(2, 16, 128),
-            vm(2, 16, 128),
-            vm(3, 8, 128),
-            vm(23, 8, 128),
-            dma(2), dma(CHUNKS),
-            dma(2, CHUNKS), dma(2, CHUNKS), dma(2, CHUNKS), dma(2, CHUNKS),
-            dma(2, CHUNKS), dma(2, CHUNKS),
-            dma(2), dma(2), dma(2), dma(2), dma(2), dma(2), dma(2), dma(2),
+            vm(2, 2, 8, 128),
+            vm(2, 2, 8, 128),
+            vm(3, 1, 128),
+            vm(23, 1, 128),
+            dma(2),
+            dma(2, n), dma(2, n), dma(2, n), dma(2, n), dma(2, n), dma(2, n),
+            dma(2), dma(2), dma(2), dma(2), dma(2), dma(2), dma(2), dma(2), dma(2), dma(2),
             dma(23), dma(23),
         ],
-        compiler_params=pltpu.CompilerParams(collective_id=0, has_side_effects=True),
-        name="bootstrap",
-    )(test_vectors, conductivity)
+        compiler_params=pltpu.CompilerParams(
+            collective_id=0, has_side_effects=True, vmem_limit_bytes=24 << 20
+        ),
+        name="relax",
+    )(*[pltpu.with_memory_space_constraint(x, pltpu.HBM) for x in (test_vectors, conductivity)])
+    return pl.pallas_call(
+        finish,
+        out_shape=(shape(4, 4, ROWS, ACROSS), shape(10, 1, 24, 64)),
+        in_specs=[in_vmem] * 4,
+        out_specs=(anywhere, anywhere),
+        scratch_shapes=[
+            vm(10, 32, 2 * ACROSS),
+            vm(4, 4, ROWS, ACROSS),
+            vm(10, 1, 24, 64),
+            dma(4),
+            pltpu.SemaphoreType.DMA,
+        ],
+        compiler_params=pltpu.CompilerParams(vmem_limit_bytes=16 << 20),
+        name="finish",
+    )(*staged)
 
 
 def solution(mesh):

time: 71.8 us -> 65.2 us (0.908)
  local copies, waits for them, and re-layouts: 3.38 us -> 0 us
  Pallas kernels: 67.6 us -> 64.4 us
    unnamed x4 -> x0, local copies, waits for them, and re-layouts: 3.38 us -> none
    pallas_call x1 -> x2, Pallas kernels: 67.6 us -> 64.4 us  [the longest x1 62.3 us: body(): pl.pallas_call(kernel, out_shape=(shape(4, 4, ROWS, ACROSS), shape(2, EAR...]
where the time goes in v2:
time: 65.2 us; the launch traced here: 65 us
  Pallas kernels  64.4 us (99%)
    pallas_call x1, Pallas kernels, body(): pl.pallas_call(kernel, out_shape=(shape(4, 4, ROWS, ACROSS), shape(2, EAR...  62.3 us
    pallas_call x1, Pallas kernels, body(): pl.pallas_call(finish, out_shape=(shape(4, 4, ROWS, ACROSS), shape(10, 1,...  2.15 us

profile of v2, /device:TPU:1, one launch (start us, length us, event | category | flops | bytes accessed | tf_op | source)
XLA Modules:
  0.0 65.0 jit_solution(15597315621509135586)
XLA Ops:
  0.6 62.3 %relax.1 = (f32[4,4,96,256]{3,2,1,0:T(8,128)S(1)}, f32[2,88,128]{2,1,0:T(8,128)S(1)}, f32[2,40,128]{2,1,0:T(8,128)S(1)}, f32[8,128]{1,0:T(8,128)S(1)}) custom-call(f32[4,4,96,256]{3,2,1,0:T(8,128)} %tv_hbm.1, f32[4,96,256]{2,1,0:T(8,128)} %k_hbm.1), custom_call_target="tpu_custom_call" | custom-call | tf_op jit(solution)/shard_map/relax/pallas_call | solution.py:461
  62.9 2.1 %finish.1 = (f32[4,4,96,256]{3,2,1,0:T(8,128)}, f32[10,1,24,64]{3,2,1,0:T(8,128)}) custom-call(f32[4,4,96,256]{3,2,1,0:T(8,128)S(1)} %get-tuple-element.6.r, f32[2,88,128]{2,1,0:T(8,128)S(1)} %get-tuple-element.7.gram_early, f32[2,40,128]{2,1,0:T(8,128)S(1)} %get-tuple-element.8.gram_late, f32[8,128]{1,0:T(8,128)S(1)} %get-tuple-element.9.total_ref), custom_call_target="tpu_custom_call" | custom-call | tf_op jit(solution)/shard_map/finish/pallas_call | solution.py:504

commit v3 on v2

v3 whole, which is shorter than its diff:
```python
import functools

import jax
import jax.numpy as jnp
from jax import lax
from jax.experimental import pallas as pl
from jax.experimental.pallas import tpu as pltpu
from jax.sharding import PartitionSpec as P

MESH = pl.DeviceIdType.MESH
F32 = jnp.float32
KEEP = 1.0 / 3.0
STEP = 2.0 / 3.0
PAIRS = ((0, 0), (0, 1), (0, 2), (0, 3), (1, 1), (1, 2), (1, 3), (2, 2), (2, 3), (3, 3))
AT = {pair: i for i, pair in enumerate(PAIRS)}
BF16 = jnp.bfloat16
ROWS = 96
ACROSS = 256
PAD = 8
TILES = ROWS // 8
CHUNKS = ((0, 3), (8, 4), (3, 3), (6, 2))
EARLY = 88
LATE = 40
N_GZ = 64
N_GY = 4
CELLS = 256 * 384 * 256


def device(z, y, x_hi, x_lo, core):
    return (z * 8 + y * 2 + x_hi, x_lo * 2 + core)


def sum_partners():
    gz, gy = lax.axis_index("gz"), lax.axis_index("gy")
    z, y, x_hi = gz // 8, lax.rem(gz, 8) // 2, lax.rem(gz, 2)
    x_lo, core = gy // 2, lax.rem(gy, 2)
    column = [
        device(lax.rem(z + dz, 8), y, x_hi, x_lo, lax.rem(core + dc, 2))
        for dz in (4, 3, 5, 2, 6, 1, 7, 0)
        for dc in (1, 0)
        if dz or dc
    ]
    plane = [
        device(z, lax.rem(y + dy, 4), lax.rem(x_hi + dh, 2), lax.rem(x_lo + dl, 2), core)
        for dy in (2, 1, 3, 0)
        for dh in (1, 0)
        for dl in (0, 1)
        if dy or dh or dl
    ]
    return column, plane


GROUP = 15


def spans():
    return [(c, tile * 8, tiles * 8) for c, (tile, tiles) in enumerate(CHUNKS)]


def split_dot(x, table):
    high = x.astype(BF16)
    rest = x - high.astype(F32)
    middle = rest.astype(BF16)
    low = (rest - middle.astype(F32)).astype(BF16)
    one = jnp.dot(low, table, preferred_element_type=F32)
    two = jnp.dot(middle, table, preferred_element_type=F32)
    return (one + two) + jnp.dot(high, table, preferred_element_type=F32)


def kernel(
    tv_hbm, k_hbm, r, gram_early, gram_late, total_ref, expand_ref,
    tv, kc, hz, f, fz, wn, prod, sum_early, sum_late,
    mine_early, mine_late, from_early, from_late,
    ysend, yrecv, fysend, fyrecv, edges, esend, erecv, ends, from_ends, sum_send, sum_recv,
    load_sem, a_send, a_recv, b_send, b_recv, pair_send, pair_recv, s_send, s_recv,
):
    gz, gy = lax.axis_index("gz"), lax.axis_index("gy")
    z_dev = (
        (lax.rem(gz + N_GZ - 1, N_GZ), gy),
        (lax.rem(gz + 1, N_GZ), gy),
    )
    y_dev = (
        (gz, lax.rem(gy + N_GY - 1, N_GY)),
        (gz, lax.rem(gy + 1, N_GY)),
    )
    partners = sum_partners()

    def remote(src, dst, send_sem, recv_sem, to):
        return pltpu.make_async_remote_copy(
            src_ref=src, dst_ref=dst, send_sem=send_sem, recv_sem=recv_sem,
            device_id=to, device_id_type=MESH,
        )

    def wait(sem, whole):
        pltpu.make_async_copy(whole, whole, sem).wait()

    def swap(at, sources, landing, to):
        for side in range(2):
            remote(
                sources.at[side], landing.at[1 - side], pair_send.at[at], pair_recv.at[at], to[side]
            ).start()

    loads = [
        pltpu.make_async_copy(tv_hbm, tv.at[:, :, pl.ds(PAD, ROWS), :], load_sem.at[0]),
        pltpu.make_async_copy(k_hbm, kc.at[:, pl.ds(PAD, ROWS), :], load_sem.at[1]),
    ]
    for copy in loads:
        copy.start()

    barrier = pltpu.get_barrier_semaphore()
    greeted = list(z_dev) + list(y_dev) + [d for group in partners for d in group]
    for to in greeted:
        pl.semaphore_signal(barrier, inc=1, device_id=to, device_id_type=MESH)

    pl.semaphore_wait(barrier, len(greeted))

    face = (0, 3)

    def send_faces(c, start, count):
        rows = pl.ds(start, count)
        for side in range(2):
            remote(
                k_hbm.at[face[side], rows, :], hz.at[1 - side, 4, rows, :],
                a_send.at[c], a_recv.at[c], z_dev[side],
            ).start()
            remote(
                tv_hbm.at[:, face[side], rows, :], hz.at[1 - side, pl.ds(0, 4), rows, :],
                a_send.at[c], a_recv.at[c], z_dev[side],
            ).start()

    send_faces(*spans()[0])
    for copy in loads:
        copy.wait()
    for side, row in ((0, PAD), (1, PAD + ROWS - 1)):
        for p in range(4):
            for v in range(4):
                ysend[side, pl.ds(v * 4 + p, 1), :] = tv[v, p, pl.ds(row, 1), :]
            ysend[side, pl.ds(16 + p, 1), :] = kc[p, pl.ds(row, 1), :]
        ysend[side, pl.ds(20, 4), :] = jnp.zeros((4, ACROSS), F32)
    swap(0, ysend, yrecv, y_dev)
    for span in spans()[1:]:
        send_faces(*span)

    for field in range(20):
        for side in range(2):
            prod[field, side, pl.ds(ROWS, 8), :] = jnp.zeros((8, 128), F32)
    for half in range(2):
        edges[half, 1] = jnp.zeros((8, 128), F32)
        for part in range(2):
            sum_early[half, part, pl.ds(80, 8), :] = jnp.zeros((8, ACROSS), F32)
    across = lax.broadcasted_iota(jnp.int32, (256, 2 * ACROSS), 1)
    owner = (((across + (ACROSS - 2)) & (ACROSS - 1)) >> 2) + ((across >> 8) << 6)
    source = lax.broadcasted_iota(jnp.int32, (256, 2 * ACROSS), 0) & 127
    expand_ref[...] = (source == owner).astype(F32).astype(BF16)

    wait(pair_recv.at[0], yrecv)
    for side, row in ((0, PAD - 1), (1, PAD + ROWS)):
        for p in range(4):
            for v in range(4):
                tv[v, p, pl.ds(row, 1), :] = yrecv[side, pl.ds(v * 4 + p, 1), :]
            kc[p, pl.ds(row, 1), :] = yrecv[side, pl.ds(16 + p, 1), :]

    def left(x):
        return pltpu.roll(x, 1, 1)

    def right(x):
        return pltpu.roll(x, ACROSS - 1, 1)

    def weights(t, p):
        at = t * 8
        here = kc[p, pl.ds(at + PAD, 8), :]
        near = (
            kc[p + 1, pl.ds(at + PAD, 8), :] if p < 3 else hz[1, 4, pl.ds(at, 8), :],
            kc[p - 1, pl.ds(at + PAD, 8), :] if p > 0 else hz[0, 4, pl.ds(at, 8), :],
            kc[p, pl.ds(at + PAD + 1, 8), :],
            kc[p, pl.ds(at + PAD - 1, 8), :],
            right(here),
            left(here),
        )
        parts = [n / (here + n) for n in near]
        total = ((parts[0] + parts[1]) + (parts[2] + parts[3])) + (parts[4] + parts[5])
        norm = STEP / total
        for i in range(6):
            wn[i, p, pl.ds(at, 8), :] = parts[i] * norm

    def relax(t, p, src, halo=None):
        at = t * 8
        w = [wn[i, p, pl.ds(at, 8), :] for i in range(6)]
        result = []
        for v in range(4):
            here = src[v, p, pl.ds(at + PAD, 8), :]
            up = src[v, p + 1, pl.ds(at + PAD, 8), :] if p < 3 else None
            down = src[v, p - 1, pl.ds(at + PAD, 8), :] if p > 0 else None
            if halo is not None and p == 3:
                up = halo[1, v, pl.ds(at, 8), :]
            if halo is not None and p == 0:
                down = halo[0, v, pl.ds(at, 8), :]
            ahead = src[v, p, pl.ds(at + PAD + 1, 8), :]
            behind = src[v, p, pl.ds(at + PAD - 1, 8), :]
            total = w[2] * ahead + w[3] * behind
            total = total + (w[4] * right(here) + w[5] * left(here))
            total = here * KEEP + total
            if up is not None:
                total = total + w[0] * up
            if down is not None:
                total = total + w[1] * down
            result.append(total)
        return result

    def first_tile(t, p):
        for v, value in enumerate(relax(t, p, tv, hz)):
            f[v, p, pl.ds(t * 8 + PAD, 8), :] = value

    def second_tile(t, p):
        for v, value in enumerate(relax(t, p, f)):
            r[v, p, pl.ds(t * 8, 8), :] = value

    def add_halo(t, half):
        rows = pl.ds(t * 8, 8)
        p = face[half]
        w = wn[1 - half, p, rows, :]
        for v in range(4):
            r[v, p, rows, :] = r[v, p, rows, :] + w * fz[half, v, rows, :]

    for t in range(TILES):
        for p in (1, 2):
            weights(t, p)
            first_tile(t, p)

    for c, start, count in spans():
        rows = pl.ds(start, count)
        wait(a_recv.at[c], hz.at[:, :, rows, :])
        for t in range(start // 8, (start + count) // 8):
            for p in face:
                weights(t, p)
                first_tile(t, p)
        for side in range(2):
            remote(
                f.at[:, face[side], pl.ds(start + PAD, count), :], fz.at[1 - side, :, rows, :],
                b_send.at[c], b_recv.at[c], z_dev[side],
            ).start()
        if c == 1:
            for side, row in ((0, PAD), (1, PAD + ROWS - 1)):
                for p in range(4):
                    for v in range(4):
                        fysend[side, pl.ds(v * 4 + p, 1), :] = f[v, p, pl.ds(row, 1), :]
            swap(1, fysend, fyrecv, y_dev)

    wait(pair_recv.at[1], fyrecv)
    for side, row in ((0, PAD - 1), (1, PAD + ROWS)):
        for p in range(4):
            for v in range(4):
                f[v, p, pl.ds(row, 1), :] = fyrecv[side, pl.ds(v * 4 + p, 1), :]
    for t in range(TILES):
        for p in range(4):
            second_tile(t, p)
    wait(pair_send.at[0], ysend)
    wait(pair_send.at[1], fysend)
    for c, start, count in spans():
        wait(a_send.at[c], hz.at[:, :, pl.ds(start, count), :])

    def group_sums(field, first_row, into, at):
        for side in range(2):
            parts = [prod[field, side, pl.ds(first_row + i, 8, stride=4), :] for i in range(4)]
            into[field // 10, (field % 10) // 5, pl.ds(at, 8), pl.ds(side * 128, 128)] = (
                (parts[0] + parts[1]) + (parts[2] + parts[3])
            )

    cell = ((lax.broadcasted_iota(jnp.int32, (ACROSS, 128), 0) + (ACROSS - 2)) & (ACROSS - 1)) >> 2
    lane = lax.broadcasted_iota(jnp.int32, (ACROSS, 128), 1)
    pick = [(cell + 64 * part == lane).astype(F32).astype(BF16) for part in range(2)]

    def pack(sums, half):
        return split_dot(sums[half, 0], pick[0]) + split_dot(sums[half, 1], pick[1])

    squares = [jnp.zeros((8, ACROSS), F32) for _ in range(4)]
    for c, start, count in spans():
        if c == len(CHUNKS) - 1:
            for field in range(20):
                n = field % 5
                group_sums(field, 2, sum_early, n * 8)
                group_sums(field, 66, sum_early, 40 + n * 8)
                for side in range(2):
                    sum_early[field // 10, (field % 10) // 5, pl.ds(80 + n, 1), pl.ds(side * 128, 128)] = (
                        prod[field, side, pl.ds(0, 1), :] + prod[field, side, pl.ds(1, 1), :]
                    )
            for half in range(2):
                packed = pack(sum_early, half)
                mine_early[half] = packed[:80]
                edges[half, 0] = packed[80:]
                for i in range(5):
                    edges[half, 1, pl.ds(i, 1), :] = packed[47 + 8 * i : 48 + 8 * i]
            swap(2, mine_early, from_early, z_dev)
            for half in range(2):
                esend[0, half] = edges[half, 0]
                esend[1, half] = edges[half, 1]
            swap(4, esend, erecv, y_dev)
        wait(b_recv.at[c], fz.at[:, :, pl.ds(start, count), :])
        for t in range(start // 8, (start + count) // 8):
            rows = pl.ds(t * 8, 8)
            for half in range(2):
                add_halo(t, half)
                low = [r[v, 2 * half, rows, :] for v in range(4)]
                high = [r[v, 2 * half + 1, rows, :] for v in range(4)]
                for i, (a, b) in enumerate(PAIRS):
                    value = low[a] * low[b] + high[a] * high[b]
                    prod[half * 10 + i, 0, rows, :] = value[:, :128]
                    prod[half * 10 + i, 1, rows, :] = value[:, 128:]
                    if a == b:
                        squares[a] = squares[a] + value

    def exchange(stage):
        for i, to in enumerate(partners[stage]):
            remote(
                sum_send.at[stage], sum_recv.at[stage, i], s_send.at[stage], s_recv.at[stage], to
            ).start()

    def collect(stage):
        wait(s_recv.at[stage], sum_recv.at[stage])
        total = [sum_send[stage]] + [sum_recv[stage, i] for i in range(GROUP)]
        while len(total) > 1:
            total = [total[i] + total[i + 1] for i in range(0, len(total), 2)]
        return total[0]

    stacked = [jnp.sum(q[:, :128] + q[:, 128:], axis=0, keepdims=True) for q in squares]
    stacked = jnp.concatenate(stacked + [jnp.zeros((4, 128), F32)], axis=0)
    stacked = jnp.sum(stacked, axis=1, keepdims=True)
    on_diagonal = lax.broadcasted_iota(jnp.int32, (8, 128), 0) == lax.broadcasted_iota(
        jnp.int32, (8, 128), 1
    )
    sum_send[0] = jnp.sum(jnp.where(on_diagonal, stacked, 0.0), axis=0, keepdims=True)
    exchange(0)

    for field in range(20):
        group_sums(field, 34, sum_late, (field % 5) * 8)
    for half in range(2):
        mine_late[half] = pack(sum_late, half)
    swap(3, mine_late, from_late, z_dev)
    wait(pair_recv.at[4], erecv)
    for half in range(2):
        for kind in range(2):
            ends[half, kind] = edges[half, kind] + erecv[kind, half]
    swap(5, ends, from_ends, z_dev)
    for c, start, count in spans():
        wait(b_send.at[c], fz.at[:, :, pl.ds(start, count), :])

    sum_send[1] = collect(0)
    exchange(1)

    wait(pair_recv.at[2], from_early)
    for half in range(2):
        gram_early[half, pl.ds(0, 80), :] = mine_early[half] + from_early[half]
    wait(pair_recv.at[3], from_late)
    for half in range(2):
        gram_late[half] = mine_late[half] + from_late[half]
    wait(pair_recv.at[5], from_ends)
    for half in range(2):
        gram_early[half, pl.ds(80, 8), :] = ends[half, 0] + from_ends[half, 0]
        last = ends[half, 1] + from_ends[half, 1]
        for i in range(5):
            gram_early[half, pl.ds(47 + 8 * i, 1), :] = last[i : i + 1]
    wait(pair_send.at[2], mine_early)
    wait(pair_send.at[3], mine_late)
    wait(pair_send.at[4], esend)
    wait(pair_send.at[5], ends)
    wait(s_send.at[0], sum_recv.at[0])
    total_ref[...] = jnp.broadcast_to(collect(1), (8, 128))
    wait(s_send.at[1], sum_recv.at[1])


def finish(
    r, gram_early, gram_late, total_ref, expand, out_hbm, fac_hbm, spread, out, fac, out_sem, fac_sem
):
    is_low = lax.broadcasted_iota(jnp.int32, (32, 128), 1) < 64
    lane = lax.broadcasted_iota(jnp.int32, (1, 128), 1)
    scale_row = lax.rsqrt(total_ref[0:1, :] / CELLS + 1e-06)
    scale = [
        jnp.sum(jnp.where(lane == v, scale_row, 0.0), axis=1, keepdims=True) for v in range(4)
    ]

    def groups(half, i):
        edge = jnp.broadcast_to(gram_early[half, pl.ds(80 + i, 1), :], (8, 128))
        return jnp.concatenate(
            [
                edge,
                gram_early[half, pl.ds(8 * i, 8), :],
                gram_late[half, pl.ds(8 * i, 8), :],
                gram_early[half, pl.ds(40 + 8 * i, 8), :],
            ],
            axis=0,
        )

    gram = [None] * 10
    for i in range(5):
        low, high = groups(0, i), groups(1, i)
        gram[i] = jnp.where(is_low, low, pltpu.roll(high, 64, 1))
        gram[i + 5] = jnp.where(is_low, pltpu.roll(low, 64, 1), high)

    m = {pair: gram[i] * (scale[pair[0]] * scale[pair[1]]) for i, pair in enumerate(PAIRS)}
    trace = (m[0, 0] + m[1, 1]) + (m[2, 2] + m[3, 3])
    ridge = 0.64 * (trace / 256.0 + 1e-06)
    upper, inverse = {}, []
    for i in range(4):
        for j in range(i, 4):
            value = m[i, j]
            if i == j:
                value = value + ridge
            for n in range(i):
                value = value - upper[n, i] * upper[n, j]
            if i == j:
                upper[i, i] = jnp.sqrt(value)
                inverse.append(1.0 / upper[i, i])
            else:
                upper[i, j] = value * inverse[i]
    table = [(scale[j] if i == j else upper[i, j]) * inverse[j] for i, j in PAIRS]
    table = jnp.concatenate(table, axis=0)
    high = table.astype(BF16)
    rest = table - high.astype(F32)
    middle = rest.astype(BF16)
    low = (rest - middle.astype(F32)).astype(BF16)
    wide = jnp.dot(low, expand[pl.ds(0, 128), :], preferred_element_type=F32) + jnp.dot(
        jnp.concatenate([high, middle], axis=1), expand[...], preferred_element_type=F32
    )
    spread[...] = wide.reshape(10, 32, 2 * ACROSS)
    for n, pair in enumerate(PAIRS):
        fac[n, 0] = pltpu.roll(upper[pair], 64, 1)[8:32, :64]
    fac_copy = pltpu.make_async_copy(fac, fac_hbm, fac_sem)
    fac_copy.start()

    sub = lax.broadcasted_iota(jnp.int32, (8, ACROSS), 0)
    before, after = sub < 2, sub >= 6

    def store(c):
        rows = pl.ds(pl.multiple_of(c * 24, 8), 24)
        return pltpu.make_async_copy(out.at[:, :, rows, :], out_hbm.at[:, :, rows, :], out_sem.at[c])

    @pl.loop(0, 4)
    def _(c):
        for n_tile in range(3):
            t = c * 3 + n_tile
            rows = pl.ds(pl.multiple_of(t * 8, 8), 8)
            for half in range(2):
                columns = pl.ds(half * ACROSS, ACROSS)
                field = []
                for n in range(10):
                    one, two, three = [spread[n, pl.ds(2 * t + 7 + i, 1), columns] for i in range(3)]
                    field.append(jnp.where(before, one, jnp.where(after, three, two)))
                for p in (2 * half, 2 * half + 1):
                    done_columns = []
                    for j in range(4):
                        value = r[j, p, rows, :] * field[AT[j, j]]
                        for i in range(j):
                            value = value - field[AT[i, j]] * done_columns[i]
                        done_columns.append(value)
                        out[j, p, rows, :] = value
        store(c).start()

    fac_copy.wait()
    for c in range(4):
        store(c).wait()


def body(test_vectors, conductivity):
    vm = lambda *shape: pltpu.VMEM(shape, F32)
    dma = lambda *shape: pltpu.SemaphoreType.DMA(shape)
    shape = lambda *dims: jax.ShapeDtypeStruct(dims, F32)
    in_vmem = pl.BlockSpec(memory_space=pltpu.VMEM)
    anywhere = pl.BlockSpec(memory_space=pl.ANY)
    n = len(CHUNKS)
    padded = ROWS + 2 * PAD
    staged = pl.pallas_call(
        kernel,
        out_shape=(
            shape(4, 4, ROWS, ACROSS),
            shape(2, EARLY, 128),
            shape(2, LATE, 128),
            shape(8, 128),
            jax.ShapeDtypeStruct((256, 2 * ACROSS), BF16),
        ),
        in_specs=[pl.BlockSpec(memory_space=pltpu.HBM)] * 2,
        out_specs=(in_vmem,) * 5,
        scratch_shapes=[
            vm(4, 4, padded, ACROSS),
            vm(4, padded, ACROSS),
            vm(2, 5, ROWS, ACROSS),
            vm(4, 4, padded, ACROSS),
            vm(2, 4, ROWS, ACROSS),
            vm(6, 4, ROWS, ACROSS),
            vm(20, 2, ROWS + 8, 128),
            vm(2, 2, EARLY, ACROSS),
            vm(2, 2, LATE, ACROSS),
            vm(2, EARLY - 8, 128),
            vm(2, LATE, 128),
            vm(2, EARLY - 8, 128),
            vm(2, LATE, 128),
            vm(2, 24, ACROSS),
            vm(2, 24, ACROSS),
            vm(2, 16, ACROSS),
            vm(2, 16, ACROSS),
            vm(2, 2, 8, 128),
            vm(2, 2, 8, 128),
            vm(2, 2, 8, 128),
            vm(2, 2, 8, 128),
            vm(2, 2, 8, 128),
            vm(2, 1, 128),
            vm(2, GROUP, 1, 128),
            dma(2),
            dma(n), dma(n), dma(n), dma(n), dma(6), dma(6), dma(2), dma(2),
        ],
        compiler_params=pltpu.CompilerParams(
            collective_id=0, has_side_effects=True, vmem_limit_bytes=24 << 20
        ),
        name="relax",
    )(*[pltpu.with_memory_space_constraint(x, pltpu.HBM) for x in (test_vectors, conductivity)])
    return pl.pallas_call(
        finish,
        out_shape=(shape(4, 4, ROWS, ACROSS), shape(10, 1, 24, 64)),
        in_specs=[in_vmem] * 5,
        out_specs=(anywhere, anywhere),
        scratch_shapes=[
            vm(10, 32, 2 * ACROSS),
            vm(4, 4, ROWS, ACROSS),
            vm(10, 1, 24, 64),
            dma(4),
            pltpu.SemaphoreType.DMA,
        ],
        compiler_params=pltpu.CompilerParams(vmem_limit_bytes=16 << 20),
        name="finish",
    )(*staged)


def solution(mesh):
    return jax.shard_map(
        body,
        mesh=mesh,
        in_specs=(P(None, "gz", "gy", None), P("gz", "gy", None)),
        out_specs=(P(None, "gz", "gy", None), P(None, "gz", "gy", None)),
        check_vma=False,
    )
```

time: 65.2 us -> 64.6 us (level)
  no operation moved by 1% of the time
where the time goes in v3:
time: 64.6 us; the launch traced here: 64.5 us
  Pallas kernels  63.8 us (99%)
    pallas_call x1, Pallas kernels, body(): pl.pallas_call(kernel, out_shape=(shape(4, 4, ROWS, ACROSS), shape(2, EAR...  62 us
    pallas_call x1, Pallas kernels, body(): pl.pallas_call(finish, out_shape=(shape(4, 4, ROWS, ACROSS), shape(10, 1,...  1.84 us

profile of v3, /device:TPU:1, one launch (start us, length us, event | category | flops | bytes accessed | tf_op | source)
XLA Modules:
  0.0 64.5 jit_solution(3900348023243400627)
XLA Ops:
  0.6 62.0 %relax.1 = (f32[4,4,96,256]{3,2,1,0:T(8,128)S(1)}, f32[2,88,128]{2,1,0:T(8,128)S(1)}, f32[2,40,128]{2,1,0:T(8,128)S(1)}, f32[8,128]{1,0:T(8,128)S(1)}, bf16[256,512]{1,0:T(8,128)(2,1)S(1)}) custom-call(f32[4,4,96,256]{3,2,1,0:T(8,128)} %tv_hbm.1, f32[4,96,256]{2,1,0:T(8,128)} %k_hbm.1), custom_call_target="tpu_custom_call" | custom-call | tf_op jit(solution)/shard_map/relax/pallas_call | solution.py:471
  62.6 1.8 %finish.1 = (f32[4,4,96,256]{3,2,1,0:T(8,128)}, f32[10,1,24,64]{3,2,1,0:T(8,128)}) custom-call(f32[4,4,96,256]{3,2,1,0:T(8,128)S(1)} %get-tuple-element.7.r, f32[2,88,128]{2,1,0:T(8,128)S(1)} %get-tuple-element.8.gram_early, f32[2,40,128]{2,1,0:T(8,128)S(1)} %get-tuple-element.9.gram_late, f32[8,128]{1,0:T(8,128)S(1)} %get-tuple-element.10.total_ref, ...), custom_call_target="tpu_custom_call" | custom-call | tf_op jit(solution)/shard_map/finish/pallas_call | solution.py:515

commit v4 on v3

--- a/solution.py
+++ b/solution.py
@@ -18,7 +18,7 @@
 ACROSS = 256
 PAD = 8
 TILES = ROWS // 8
-CHUNKS = ((0, 3), (8, 4), (3, 3), (6, 2))
+CHUNKS = ((0, 2), (10, 2), (8, 2), (2, 3), (5, 2), (7, 1))
 EARLY = 88
 LATE = 40
 N_GZ = 64
@@ -290,7 +290,6 @@
                 edges[half, 0] = packed[80:]
                 for i in range(5):
                     edges[half, 1, pl.ds(i, 1), :] = packed[47 + 8 * i : 48 + 8 * i]
-            swap(2, mine_early, from_early, z_dev)
             for half in range(2):
                 esend[0, half] = edges[half, 0]
                 esend[1, half] = edges[half, 1]
@@ -336,6 +335,7 @@
     for half in range(2):
         mine_late[half] = pack(sum_late, half)
     swap(3, mine_late, from_late, z_dev)
+    swap(2, mine_early, from_early, z_dev)
     wait(pair_recv.at[4], erecv)
     for half in range(2):
         for kind in range(2):

time: 64.6 us -> 63.1 us (0.977)
  Pallas kernels: 63.8 us -> 62.4 us
    pallas_call x1, Pallas kernels: 62 us -> 60.6 us  [body(): pl.pallas_call(kernel, out_shape=(shape(4, 4, ROWS, ACROSS), shape(2, EAR...]
where the time goes in v4:
time: 63.1 us; the launch traced here: 63 us
  Pallas kernels  62.4 us (99%)
  between operations  0.64 us (1%)
    pallas_call x1, Pallas kernels, body(): pl.pallas_call(kernel, out_shape=(shape(4, 4, ROWS, ACROSS), shape(2, EAR...  60.6 us
    pallas_call x1, Pallas kernels, body(): pl.pallas_call(finish, out_shape=(shape(4, 4, ROWS, ACROSS), shape(10, 1,...  1.84 us

profile of v4, /device:TPU:1, one launch (start us, length us, event | category | flops | bytes accessed | tf_op | source)
XLA Modules:
  0.0 63.0 jit_solution(17804209999191397039)
XLA Ops:
  0.6 60.6 %relax.1 = (f32[4,4,96,256]{3,2,1,0:T(8,128)S(1)}, f32[2,88,128]{2,1,0:T(8,128)S(1)}, f32[2,40,128]{2,1,0:T(8,128)S(1)}, f32[8,128]{1,0:T(8,128)S(1)}, bf16[256,512]{1,0:T(8,128)(2,1)S(1)}) custom-call(f32[4,4,96,256]{3,2,1,0:T(8,128)} %tv_hbm.1, f32[4,96,256]{2,1,0:T(8,128)} %k_hbm.1), custom_call_target="tpu_custom_call" | custom-call | tf_op jit(solution)/shard_map/relax/pallas_call | solution.py:471
  61.2 1.8 %finish.1 = (f32[4,4,96,256]{3,2,1,0:T(8,128)}, f32[10,1,24,64]{3,2,1,0:T(8,128)}) custom-call(f32[4,4,96,256]{3,2,1,0:T(8,128)S(1)} %get-tuple-element.7.r, f32[2,88,128]{2,1,0:T(8,128)S(1)} %get-tuple-element.8.gram_early, f32[2,40,128]{2,1,0:T(8,128)S(1)} %get-tuple-element.9.gram_late, f32[8,128]{1,0:T(8,128)S(1)} %get-tuple-element.10.total_ref, ...), custom_call_target="tpu_custom_call" | custom-call | tf_op jit(solution)/shard_map/finish/pallas_call | solution.py:515
